TPU v7x, 768 devices: a whole 4x8x12 slice. The times are simulated.
768 devices in a mesh: comp: 4 (over x), tile: 24 (over y, z_lo), rep: 8 (over z_hi, core).
Axes of the slice: x: 4, y: 8, z: 12 (z_hi: 4, z_lo: 3; z = z_hi * 3 + z_lo), core: 2. Of those that a mesh axis runs over, the one named last changes fastest.
Arguments:
- retarded: bfloat16 [2, 384, 2, 192, 192], P(None, ('tile', 'rep')), may hold values from -0.3125 to 0.3125
- self_energy: bfloat16 [4, 384, 2, 192, 192], P('comp', ('tile', 'rep')), may hold values from -6 to 6
- energy_of: int32 [384], replicated, may hold values from 0 to 383, each once
Outputs:
- polar: float32 [4, 384, 2, 192, 192], P('comp', 'tile', None, 'rep')
Inputs may be any that keep to these rules, and one draw needn't show every extreme that they name: `energy_of`: each of the 384 energy grid indices stands in exactly one slot.
All inputs are finite; a program needn't handle non-finite values.
Results may differ from a plain program's by a relative error of at most 0.0095.
Values may be sent and summed in bfloat16 or wider, within the bound.
No kernel may reach another device: no remote copies, remote signals or barrier semaphores. Data moves between devices by JAX's collectives and lax.ppermute only.
A program may use at most 32 MiB of HBM per device.

v0:
```python
import functools
import math

import jax
import jax.numpy as jnp
import numpy as np
from jax import lax
from jax.experimental import pallas as pl
from jax.experimental.pallas import tpu as pltpu
from jax.sharding import Mesh, PartitionSpec as P

LANES = 128
INTERPRET = False


def twiddles(count):
    steps = (2 * np.arange(count)[:, None] + 1) * np.arange(count)[None, :] % (4 * count)
    angles = steps * (math.pi / (2 * count))
    return np.cos(angles), np.sin(angles)


def batched(left_side, right_side, pattern):
    return jnp.einsum(pattern, left_side, right_side, preferred_element_type=jnp.float32)


def dot(left_side, right_side):
    return jnp.dot(left_side, right_side, preferred_element_type=jnp.float32)


def forward_sums(signal, energy, table):
    count = energy.shape[1]
    grid_index = lax.broadcasted_iota(jnp.int32, (count, count), 0)
    pick = (grid_index == energy).astype(jnp.float32).astype(jnp.bfloat16)
    ordered = dot(pick, signal).astype(jnp.bfloat16)
    return dot(table, ordered)


def forward_kernel(signal_ref, energy_ref, table_ref, out_ref):
    out_ref[...] = forward_sums(signal_ref[...], energy_ref[...], table_ref[...])


def times(left, right):
    left_re, left_im = left[:, :LANES], left[:, LANES:]
    right_re, right_im = right[:, :LANES], right[:, LANES:]
    return left_re * right_re - left_im * right_im, left_re * right_im + left_im * right_re


def correlate_kernel(sign_ref, signal_ref, energy_ref, table_ref, own_ref, back_cos_ref, back_sin_ref, out_ref, *, scale):
    count = energy_ref.shape[1]
    other = forward_sums(signal_ref[...], energy_ref[...], table_ref[...])
    own_cos, own_sin = own_ref[:count, :], own_ref[count:, :]
    other_cos, other_sin = other[:count], other[count:]
    sign = sign_ref[0]
    even_parts = [a + b for a, b in zip(times(own_cos, other_cos), times(own_sin, other_sin))]
    odd_parts = [(a - b) * sign for a, b in zip(times(own_sin, other_cos), times(own_cos, other_sin))]
    even = dot(back_cos_ref[...], jnp.concatenate(even_parts, axis=1).astype(jnp.bfloat16))
    odd = dot(back_sin_ref[...], jnp.concatenate(odd_parts, axis=1).astype(jnp.bfloat16))
    for member, total in enumerate((even + odd, even - odd)):
        out_ref[member, :, :LANES] = (total[:, LANES:] * scale).astype(out_ref.dtype)
        out_ref[member, :, LANES:] = (total[:, :LANES] * -scale).astype(out_ref.dtype)


def body(retarded, self_energy, energy_of, *, sizes):
    tile_count, rep_count = sizes
    member = lax.axis_index("mem")
    momentum = lax.axis_index("pair")
    green_matrix = lax.dynamic_index_in_dim(retarded, momentum, 0, keepdims=False)
    sigma_matrix = self_energy[0]
    green_re, green_im = (green_matrix[:, 0], green_matrix[:, 1])
    sigma_re, sigma_im = (sigma_matrix[:, 0], sigma_matrix[:, 1])
    left_re = (
        batched(green_re, sigma_re, "eik,ekj->eij") - batched(green_im, sigma_im, "eik,ekj->eij")
    ).astype(jnp.bfloat16)
    left_im = (
        batched(green_re, sigma_im, "eik,ekj->eij") + batched(green_im, sigma_re, "eik,ekj->eij")
    ).astype(jnp.bfloat16)
    out_re = batched(left_re, green_re, "eik,ejk->eij") + batched(left_im, green_im, "eik,ejk->eij")
    out_im = batched(left_im, green_re, "eik,ejk->eij") - batched(left_re, green_im, "eik,ejk->eij")
    stacked = jnp.stack([out_re, out_im]).astype(jnp.bfloat16)
    stacked = jnp.where(member == 1, jnp.swapaxes(stacked, 2, 3), stacked)

    energy_dev, order = stacked.shape[1], stacked.shape[2]
    slot_count = energy_of.shape[0]
    half = order // 2
    blocks = stacked.reshape(2, energy_dev, rep_count, tile_count, 2, half)
    blocks = blocks.transpose(3, 2, 1, 4, 0, 5).reshape(tile_count * rep_count, energy_dev, 2 * order)
    gathered = lax.all_to_all(blocks, ("tile", "rep"), split_axis=0, concat_axis=0, tiled=True)
    halves = gathered.reshape(slot_count, 2, 2, half)
    away = lax.dynamic_index_in_dim(halves, 1 - member, 1, keepdims=False)
    partner = lax.ppermute(away.reshape(slot_count, order), "mem", [(0, 1), (1, 0)]).reshape(slot_count, 2, half)
    here = lax.dynamic_index_in_dim(halves, member, 1, keepdims=False)

    def spread(part):
        return jnp.pad(part, ((0, 0), (0, 0), (0, LANES - half))).reshape(slot_count, 2 * LANES)

    cos_part, sin_part = twiddles(slot_count)
    table = jnp.asarray(np.concatenate([cos_part, sin_part]), jnp.bfloat16)
    back_cos, back_sin = jnp.asarray(cos_part.T, jnp.bfloat16), jnp.asarray(sin_part.T, jnp.bfloat16)
    energy = energy_of.reshape(1, slot_count)
    own = pl.pallas_call(
        forward_kernel,
        out_shape=jax.ShapeDtypeStruct((2 * slot_count, 2 * LANES), jnp.float32),
        interpret=INTERPRET,
        name="own_sums",
    )(spread(here), energy, table)
    sign = (1 - 2 * member).astype(jnp.float32).reshape(1)
    vmem = pl.BlockSpec(memory_space=pltpu.VMEM)
    polar = pl.pallas_call(
        functools.partial(correlate_kernel, scale=2.0 / (2 * slot_count * math.sqrt(slot_count))),
        out_shape=jax.ShapeDtypeStruct((2, slot_count, 2 * LANES), jnp.bfloat16),
        in_specs=[pl.BlockSpec(memory_space=pltpu.SMEM)] + [vmem] * 6,
        interpret=INTERPRET,
        name="correlate",
    )(sign, spread(partner), energy, table, own, back_cos, back_sin)
    lag_count = slot_count // tile_count
    packed = polar.reshape(2, slot_count, 2, LANES)[..., :half].reshape(2 * tile_count, lag_count // 2, 2 * order)
    regrouped = lax.all_to_all(packed, ("mem", "tile"), split_axis=0, concat_axis=0, tiled=True)
    regrouped = regrouped.reshape(2, tile_count, lag_count, 2, half).transpose(2, 3, 1, 0, 4)
    return regrouped.reshape(1, lag_count, 2, tile_count, order).astype(jnp.float32)


def solution(mesh):
    comp, tile, rep = mesh.devices.shape
    split = Mesh(mesh.devices.reshape(2, comp // 2, tile, rep), ("pair", "mem", "tile", "rep"))
    placed = (
        P(None, ("tile", "rep"), None, None, None),
        P(("pair", "mem"), ("tile", "rep"), None, None, None),
        P(),
    )
    return jax.shard_map(
        functools.partial(body, sizes=(tile, rep)),
        mesh=split,
        in_specs=placed,
        out_specs=P(("pair", "mem"), "tile", None, "rep", None),
        check_vma=False,
    )
```

profile of v0, /device:TPU:8, one launch (start us, length us, event | category | flops | bytes accessed | tf_op | source)
XLA Modules:
  0.0 83.7 jit_solution(18315633597384517227)
XLA Ops:
  0.0 0.0 copy-start
  0.0 1.1 %copy-done = bf16[2,2,2,192,192]{4,3,2,1,0:T(8,128)(2,1)S(1)} copy-done((bf16[2,2,2,192,192]{4,3,2,1,0:T(8,128)(2,1)S(1)}, bf16[2,2,2,192,192]{4,3,2,1,0:T(8,128)(2,1)}, u32[]{:S(2)}) %copy-start) | copy-done | bytes 589848
  1.1 1.0 %copy_bitcast_fusion.1 = (bf16[2,2,192,192]{3,2,0,1:T(8,128)(2,1)S(1)}, bf16[2,2,192,192]{3,2,0,1:T(8,128)(2,1)S(1)}) fusion(bf16[1,2,2,192,192]{4,3,2,1,0:T(8,128)(2,1)} %param.7, bf16[2,2,2,192,192]{4,3,2,1,0:T(8,128)(2,1)S(1)} %copy-done, s32[]{:T(128)S(6)} %select_n.20), kind=kLoop, calls=%fused_computation.13 | loop fusion | bytes 1277956 | tf_op jit(solution)/shard_map/squeeze | solution.py:68
  2.2 0.2 fusion.6
  2.4 0.2 fusion.7
  2.6 0.2 fusion
  2.8 0.2 fusion.9
  3.1 0.2 fusion.1
  3.3 0.2 fusion.8
  3.5 0.2 fusion.5
  3.7 0.2 fusion.4
  4.0 0.1 pad_maximum_fusion
  4.1 0.2 copy.27
  4.3 0.1 bitcast_select_fusion
  4.4 0.2 reshape.53
  4.6 0.6 copy.39
  5.2 0.3 reshape.54
  5.5 1.0 %copy.29 = bf16[192,2,384]{2,1,0:T(2,128)(2,1)} copy(bf16[192,2,384]{2,0,1:T(8,128)(2,1)S(1)} %reshape.54) | data formatting | bytes 589824 | tf_op jit(solution)/shard_map/reshape | solution.py:86
  6.5 23.0 %all-to-all-start = ((bf16[192,2,384]{2,1,0:T(2,128)(2,1)}), bf16[192,2,384]{2,1,0:T(2,128)(2,1)S(1)}, u32[]{:S(2)}, u32[]{:S(2)}) async-start(bf16[192,2,384]{2,1,0:T(2,128)(2,1)} %copy.29), calls=%async_computation | async-start | bytes 589824 | tf_op jit(solution)/shard_map/all_to_all | solution.py:87
  29.5 20.1 %all-to-all-done = bf16[192,2,384]{2,1,0:T(2,128)(2,1)S(1)} async-done(((bf16[192,2,384]{2,1,0:T(2,128)(2,1)}), bf16[192,2,384]{2,1,0:T(2,128)(2,1)S(1)}, u32[]{:S(2)}, u32[]{:S(2)}) %all-to-all-start) | async-done | bytes 294944 | tf_op jit(solution)/shard_map/all_to_all | solution.py:87
  49.6 0.3 reshape.55
  49.9 0.3 dynamic-slice_bitcast_fusion
  50.2 0.2 copy.30
  50.4 0.0 copy-start.1
  50.4 3.4 %collective-permute-start = (bf16[384,192]{0,1:T(8,128)(2,1)S(1)}, bf16[384,192]{0,1:T(8,128)(2,1)S(1)}, u32[]{:S(2)}, u32[]{:S(2)}) collective-permute-start(bf16[384,192]{0,1:T(8,128)(2,1)S(1)} %bitcast.60), channel_id=1, source_target_pairs={{0,192},{192,0},{1,193},{193,1},{2,194},{194,2},{3,195},{195,3},{4... | collective-permute-start | bytes 442376 | tf_op jit(solution)/shard_map/ppermute | solution.py:90
  53.8 0.0 copy-done.1
  53.8 0.6 reshape.59.energy_ref
  54.4 0.2 pad.8
  54.6 0.7 copy.40
  55.3 2.8 %own_sums.1.own_ref = f32[768,256]{1,0:T(8,128)} custom-call(bf16[384,256]{1,0:T(8,128)(2,1)} %bitcast.56, s32[1,384]{1,0:T(1,128)} %reshape.59.energy_ref, bf16[768,384]{1,0:T(8,128)(2,1)} %constant.34.clone.table_ref), custom_call_target="tpu_custom_call" | custom-call | tf_op jit(solution)/shard_map/own_sums/pallas_call | solution.py:100
  58.1 0.1 collective-permute-done
  58.1 0.8 copy.33.signal_ref
  59.0 3.5 %correlate.1 = bf16[2,384,256]{2,1,0:T(8,128)(2,1)} custom-call(f32[1]{0:T(128)} %bitcast.sign_ref, bf16[384,256]{1,0:T(8,128)(2,1)} %copy.33.signal_ref, s32[1,384]{1,0:T(1,128)} %reshape.59.energy_ref, bf16[768,384]{1,0:T(8,128)(2,1)} %constant.34.clone.table_ref, f32[768,256]{1,0:T(8,128)} %own_sums.1.own_ref, ...), custom_call_target="tpu_custom_call" | custom-call | tf_op jit(solution)/shard_map/correlate/pallas_call | solution.py:108
  62.5 1.1 %reshape.61 = bf16[2,384,2,128]{3,2,1,0:T(2,128)(2,1)S(1)} reshape(bf16[2,384,256]{2,1,0:T(8,128)(2,1)} %correlate.1) | data formatting | bytes 786432 | tf_op jit(solution)/shard_map/reshape | solution.py:116
  63.6 0.3 reshape.62
  63.9 16.9 %all_to_all.10 = bf16[48,8,384]{2,1,0:T(8,128)(2,1)S(1)} all-to-all(bf16[48,8,384]{2,1,0:T(8,128)(2,1)S(1)} %reshape.62), channel_id=1, replica_groups=mesh['pair'=2,'mem'=2,'tile'=24,'rep'=8] {'mem','tile'}, dimensions={0} | all-to-all | bytes 589824 | tf_op jit(solution)/shard_map/all_to_all | solution.py:117
  80.8 0.9 %reshape.64 = f32[2,24,16,2,96]{4,3,2,1,0:T(2,128)S(1)} reshape(bf16[48,8,384]{2,1,0:T(8,128)(2,1)S(1)} %all_to_all.10) | data formatting | bytes 884736 | tf_op jit(solution)/shard_map/convert_element_type | solution.py:119
  81.7 0.6 copy.32
  82.3 1.3 %reshape.63 = f32[1,16,2,24,192]{4,3,2,1,0:T(8,128)} reshape(f32[16,2,24,2,96]{4,3,2,1,0:T(2,128)S(1)} %copy.32) | data formatting | bytes 1179648 | tf_op jit(solution)/shard_map/convert_element_type | solution.py:119
  (1 shorter events, 0.0 us)
Async XLA Ops:
  0.0 1.1 %copy-start = (bf16[2,2,2,192,192]{4,3,2,1,0:T(8,128)(2,1)S(1)}, bf16[2,2,2,192,192]{4,3,2,1,0:T(8,128)(2,1)}, u32[]{:S(2)}) copy-start(bf16[2,2,2,192,192]{4,3,2,1,0:T(8,128)(2,1)} %param.6) | copy-start | bytes 1769476
  6.5 43.1 %all-to-all-start = ((bf16[192,2,384]{2,1,0:T(2,128)(2,1)}), bf16[192,2,384]{2,1,0:T(2,128)(2,1)S(1)}, u32[]{:S(2)}, u32[]{:S(2)}) async-start(bf16[192,2,384]{2,1,0:T(2,128)(2,1)} %copy.29), calls=%async_computation | async-start | bytes 589824 | tf_op jit(solution)/shard_map/all_to_all | solution.py:87
  50.4 3.4 %copy-start.1 = (s32[384]{0:T(512)S(1)}, s32[384]{0:T(512)}, u32[]{:S(2)}) copy-start(s32[384]{0:T(512)} %param.8) | copy-start | bytes 4612
  50.4 7.8 %collective-permute-start = (bf16[384,192]{0,1:T(8,128)(2,1)S(1)}, bf16[384,192]{0,1:T(8,128)(2,1)S(1)}, u32[]{:S(2)}, u32[]{:S(2)}) collective-permute-start(bf16[384,192]{0,1:T(8,128)(2,1)S(1)} %bitcast.60), channel_id=1, source_target_pairs={{0,192},{192,0},{1,193},{193,1},{2,194},{194,2},{3,195},{195,3},{4... | collective-permute-start | bytes 442376 | tf_op jit(solution)/shard_map/ppermute | solution.py:90
where the time goes:
time: 84.1 us; the launch traced here: 83.7 us
  starting transfers between devices  26.4 us (31%)
  waiting for transfers between devices  20.2 us (24%)
  blocking collectives  16.9 us (20%)
  local copies, waits for them, and re-layouts  11.8 us (14%)
  Pallas kernels  6.36 us (8%)
  matrix products  1.73 us (2%)
    all_to_all x1, starting transfers between devices, body(): lax.all_to_all(blocks, ('tile', 'rep'), split_axis=0, concat_axis=0, tile...  23 us
    all_to_all x1, waiting for transfers between devices, body(): lax.all_to_all(blocks, ('tile', 'rep'), split_axis=0, concat_axis=0, tile...  20.1 us
    all_to_all x1, blocking collectives, body(): lax.all_to_all(packed, ('mem', 'tile'), split_axis=0, concat_axis=0, tile...  16.9 us
    pallas_call x1, Pallas kernels, body(): pl.pallas_call(functools.partial(correlate_kernel, scale=2.0 / (2 * slot_...  3.55 us
    ppermute x1, starting transfers between devices, body(): lax.ppermute(away.reshape(slot_count, order), 'mem', [(0, 1), (1, 0)])  3.39 us
    convert_element_type x3, local copies, waits for them, and re-layouts, body(): regrouped.reshape(1, lag_count, 2, tile_count, order).astype(jnp.float32)  2.83 us
    pallas_call x1, Pallas kernels, body(): pl.pallas_call(forward_kernel, out_shape=jax.ShapeDtypeStruct((2 * slot_c...  2.81 us
    unnamed x5, local copies, waits for them, and re-layouts  1.83 us
  transfers between devices with their start and end apart: 2, of which 2 were waited for; matrix products, arithmetic and copies ran while one was open for 2% of the time, Pallas kernels for 3%

commit v1 on v0

v1 whole, which is shorter than its diff:
```python
import functools
import math

import jax
import jax.numpy as jnp
import numpy as np
from jax import lax
from jax.experimental import pallas as pl
from jax.experimental.pallas import tpu as pltpu
from jax.sharding import Mesh, PartitionSpec as P

LANES = 128
INTERPRET = False


def twiddles(count):
    steps = (2 * np.arange(count)[:, None] + 1) * np.arange(count)[None, :] % (4 * count)
    angles = steps * (math.pi / (2 * count))
    return np.cos(angles), np.sin(angles)


def dot(left_side, right_side):
    return jnp.dot(left_side, right_side, preferred_element_type=jnp.float32)


def dot_rows(left_side, right_side):
    return lax.dot_general(left_side, right_side, (((1,), (1,)), ((), ())), preferred_element_type=jnp.float32)


def one_hot(condition):
    return jnp.where(condition, 1.0, 0.0).astype(jnp.bfloat16)


def triple_kernel(place_ref, retarded_ref, self_energy_ref, out_ref, green_ref, sigma_ref, left_ref, right_ref, sems, *, sizes):
    tile_count, rep_count = sizes
    energies, _, order, _ = green_ref.shape
    half = order // 2
    copies = []
    for e in range(energies):
        pair = (
            pltpu.make_async_copy(retarded_ref.at[place_ref[0], e], green_ref.at[e], sems.at[e, 0]),
            pltpu.make_async_copy(self_energy_ref.at[0, e], sigma_ref.at[e], sems.at[e, 1]),
        )
        for copy in pair:
            copy.start()
        copies.append(pair)
    target = lax.broadcasted_iota(jnp.int32, (2 * order, 2 * order), 0)
    source = lax.broadcasted_iota(jnp.int32, (2 * order, 2 * order), 1)
    device, side = target >> 1, target & 1
    row = (device & (rep_count - 1)) * tile_count + (device >> (rep_count.bit_length() - 1))
    arrange = one_hot(source == side * order + row)
    sides = ([], [])
    for e in range(energies):
        for copy in copies[e]:
            copy.wait()
        green_re, green_im = green_ref[e, 0], green_ref[e, 1]
        sigma_re, sigma_im = sigma_ref[e, 0], sigma_ref[e, 1]
        cross_re = (dot(green_re, sigma_re) - dot(green_im, sigma_im)).astype(jnp.bfloat16)
        cross_im = (dot(green_re, sigma_im) + dot(green_im, sigma_re)).astype(jnp.bfloat16)

        def set_sides(left_re, left_im, right_re, right_im, conj, own):
            left_ref[0], left_ref[1] = left_re, left_im
            for side, start in enumerate((own * half, (1 - own) * half)):
                re, im = right_re[start : start + half], right_im[start : start + half]
                right_ref[side, 0, :half], right_ref[side, 0, half:] = re, -im if conj else im
                right_ref[side, 1, :half], right_ref[side, 1, half:] = im, re if conj else -re

        @pl.when(place_ref[1] == 0)
        def _():
            set_sides(cross_re, cross_im, green_re, green_im, True, 0)

        @pl.when(place_ref[1] == 1)
        def _():
            set_sides(green_re, green_im, cross_re, cross_im, False, 1)

        for side in range(2):
            sides[side].append(
                dot_rows(left_ref[0], right_ref[side, 0]) + dot_rows(left_ref[1], right_ref[side, 1])
            )
    stacked = jnp.concatenate([jnp.concatenate(s, axis=1) for s in sides], axis=0).astype(jnp.bfloat16)
    out_ref[...] = dot(arrange, stacked).astype(jnp.bfloat16)


def forward_sums(signal, energy, table, ordered_ref):
    energies, devices = energy.shape
    half = signal.shape[1] // (2 * energies)
    grid_index = lax.broadcasted_iota(jnp.int32, (energies * devices, devices), 0)
    picks = [one_hot(grid_index == energy[e : e + 1]) for e in range(energies)]
    ordered_ref[...] = jnp.zeros(ordered_ref.shape, ordered_ref.dtype)
    for part in range(2):
        total = None
        for e in range(energies):
            start = (2 * e + part) * half
            term = dot(picks[e], signal[:, start : start + half])
            total = term if total is None else total + term
        ordered_ref[:, part * LANES : part * LANES + half] = total.astype(jnp.bfloat16)
    return dot(table, ordered_ref[...])


def forward_kernel(signal_ref, energy_ref, table_ref, out_ref, ordered_ref):
    out_ref[...] = forward_sums(signal_ref[...], energy_ref[...], table_ref[...], ordered_ref)


def times(left, right):
    left_re, left_im = left[:, :LANES], left[:, LANES:]
    right_re, right_im = right[:, :LANES], right[:, LANES:]
    return left_re * right_re - left_im * right_im, left_re * right_im + left_im * right_re


def correlate_kernel(
    sign_ref, signal_ref, energy_ref, table_ref, own_ref, back_cos_ref, back_sin_ref, out_ref, ordered_ref, *, scale
):
    count = ordered_ref.shape[0]
    half = signal_ref.shape[1] // 4
    other = forward_sums(signal_ref[...], energy_ref[...], table_ref[...], ordered_ref)
    own_cos, own_sin = own_ref[:count, :], own_ref[count:, :]
    other_cos, other_sin = other[:count], other[count:]
    sign = sign_ref[0]
    even_parts = [a + b for a, b in zip(times(own_cos, other_cos), times(own_sin, other_sin))]
    odd_parts = [(a - b) * sign for a, b in zip(times(own_sin, other_cos), times(own_cos, other_sin))]
    even = dot(back_cos_ref[...], jnp.concatenate(even_parts, axis=1).astype(jnp.bfloat16))
    odd = dot(back_sin_ref[...], jnp.concatenate(odd_parts, axis=1).astype(jnp.bfloat16))
    rows = count // 2
    for member, total in enumerate((even + odd, even - odd)):
        re = total[:, LANES : LANES + half] * scale
        im = total[:, :half] * -scale
        out_ref[member] = jnp.concatenate([re[:rows], im[:rows], re[rows:], im[rows:]], axis=1).astype(out_ref.dtype)


def on_chip(array):
    return pltpu.with_memory_space_constraint(array, pltpu.VMEM) if not INTERPRET else array


def on_chip_out(shape, dtype):
    return pltpu.VMEM(shape, dtype) if not INTERPRET else jax.ShapeDtypeStruct(shape, dtype)


def body(retarded, self_energy, energy_of, *, sizes):
    tile_count, rep_count = sizes
    device_count = tile_count * rep_count
    member = lax.axis_index("mem")
    momentum = lax.axis_index("pair")
    energies, order = retarded.shape[1], retarded.shape[3]
    half = order // 2
    slot_count = energy_of.shape[0]
    in_vmem = pl.BlockSpec(memory_space=pltpu.VMEM)
    in_smem = pl.BlockSpec(memory_space=pltpu.SMEM)
    in_place = pl.BlockSpec(memory_space=pl.ANY)
    blocks = pl.pallas_call(
        functools.partial(triple_kernel, sizes=sizes),
        out_shape=on_chip_out((2 * device_count, 2 * energies * half), jnp.bfloat16),
        in_specs=[in_smem, in_place, in_place],
        out_specs=in_vmem,
        scratch_shapes=[
            pltpu.VMEM((energies, 2, order, order), jnp.bfloat16),
            pltpu.VMEM((energies, 2, order, order), jnp.bfloat16),
            pltpu.VMEM((2, order, order), jnp.bfloat16),
            pltpu.VMEM((2, 2, order, order), jnp.bfloat16),
            pltpu.SemaphoreType.DMA((energies, 2)),
        ],
        interpret=INTERPRET,
        name="triple",
    )(jnp.stack([momentum, member]), retarded, self_energy)
    blocks = blocks.reshape(device_count, 2, 2 * energies * half)
    gathered = lax.all_to_all(blocks, ("tile", "rep"), split_axis=0, concat_axis=0, tiled=True)
    partner = lax.ppermute(gathered[:, 1], "mem", [(0, 1), (1, 0)])

    cos_part, sin_part = twiddles(slot_count)
    table = on_chip(jnp.asarray(np.concatenate([cos_part, sin_part]), jnp.bfloat16))
    lag_count = slot_count // tile_count
    lags = np.arange(slot_count).reshape(tile_count, 2, lag_count // 2).transpose(1, 0, 2).reshape(-1)
    back_cos = on_chip(jnp.asarray(cos_part.T[lags], jnp.bfloat16))
    back_sin = on_chip(jnp.asarray(sin_part.T[lags], jnp.bfloat16))
    energy = on_chip(energy_of.reshape(device_count, energies).T)
    ordered = pltpu.VMEM((slot_count, 2 * LANES), jnp.bfloat16)
    own = pl.pallas_call(
        forward_kernel,
        out_shape=on_chip_out((2 * slot_count, 2 * LANES), jnp.float32),
        in_specs=[in_vmem] * 3,
        out_specs=in_vmem,
        scratch_shapes=[ordered],
        interpret=INTERPRET,
        name="own_sums",
    )(on_chip(gathered[:, 0]), energy, table)
    sign = (1 - 2 * member).astype(jnp.float32).reshape(1)
    polar = pl.pallas_call(
        functools.partial(correlate_kernel, scale=2.0 / (2 * slot_count * math.sqrt(slot_count))),
        out_shape=on_chip_out((2, slot_count // 2, 4 * half), jnp.bfloat16),
        in_specs=[in_smem] + [in_vmem] * 6,
        out_specs=in_vmem,
        scratch_shapes=[ordered],
        interpret=INTERPRET,
        name="correlate",
    )(sign, on_chip(partner), energy, table, own, back_cos, back_sin)
    packed = polar.reshape(2 * tile_count, lag_count // 2, 4 * half)
    regrouped = lax.all_to_all(packed, ("mem", "tile"), split_axis=0, concat_axis=0, tiled=True)
    regrouped = regrouped.reshape(2, tile_count, lag_count // 2, 2, 2, half).transpose(3, 2, 4, 1, 0, 5)
    return regrouped.reshape(1, lag_count, 2, tile_count, order).astype(jnp.float32)


def solution(mesh):
    comp, tile, rep = mesh.devices.shape
    split = Mesh(mesh.devices.reshape(2, comp // 2, tile, rep), ("pair", "mem", "tile", "rep"))
    placed = (
        P(None, ("tile", "rep"), None, None, None),
        P(("pair", "mem"), ("tile", "rep"), None, None, None),
        P(),
    )
    return jax.shard_map(
        functools.partial(body, sizes=(tile, rep)),
        mesh=split,
        in_specs=placed,
        out_specs=P(("pair", "mem"), "tile", None, "rep", None),
        check_vma=False,
    )
```

time: 84.1 us -> 78 us (0.927)
  blocking collectives: 16.9 us -> 59.8 us
  starting transfers between devices: 26.4 us -> 3.53 us
  waiting for transfers between devices: 20.2 us -> 2.36 us
  local copies, waits for them, and re-layouts: 11.8 us -> 4.52 us
  matrix products: 1.73 us -> 0 us
    all_to_all x0 -> x1, blocking collectives: none -> 42.8 us  [body(): lax.all_to_all(blocks, ('tile', 'rep'), split_axis=0, concat_axis=0, tile...]
    all_to_all x1 -> x0, starting transfers between devices: 23 us -> none  [body(): lax.all_to_all(blocks, ('tile', 'rep'), split_axis=0, concat_axis=0, tile...]
    all_to_all x1 -> x0, waiting for transfers between devices: 20.1 us -> none  [body(): lax.all_to_all(blocks, ('tile', 'rep'), split_axis=0, concat_axis=0, tile...]
    reshape x9 -> x3, local copies, waits for them, and re-layouts: 5.19 us -> 0.32 us  [the longest x2 0.21 us: body(): energy = on_chip(energy_of.reshape(device_count, energies).T)]
    ppermute x1, waiting for transfers between devices: 0.06 us -> 2.36 us  [body(): partner = lax.ppermute(gathered[:, 1], 'mem', [(0, 1), (1, 0)])]
    dot_general x8 -> x0, matrix products: 1.73 us -> none  [batched(): jnp.einsum(pattern, left_side, right_side, preferred_element_type=jnp.flo...]
    squeeze x2 -> x0, local copies, waits for them, and re-layouts: 1.33 us -> none  [the longest x1 1.05 us: body(): sigma_matrix = self_energy[0]]
    pallas_call x1 -> x2, Pallas kernels: 2.81 us -> 4.12 us  [the longest x1 3.32 us: body(): pl.pallas_call(functools.partial(triple_kernel, sizes=sizes), out_shape=o...]
  transfers between devices with their start and end apart: 2 -> 1, of which waited for: 2 -> 1; matrix products, arithmetic and copies ran while one was open for 2% -> 0% of each run, Pallas kernels for 3% -> 1%
where the time goes in v1:
time: 78 us; the launch traced here: 77.7 us
  blocking collectives  59.8 us (77%)
  Pallas kernels  6.82 us (9%)
  local copies, waits for them, and re-layouts  4.52 us (6%)
  starting transfers between devices  3.53 us (5%)
  waiting for transfers between devices  2.36 us (3%)
    all_to_all x1, blocking collectives, body(): lax.all_to_all(blocks, ('tile', 'rep'), split_axis=0, concat_axis=0, tile...  42.8 us
    all_to_all x1, blocking collectives, body(): lax.all_to_all(packed, ('mem', 'tile'), split_axis=0, concat_axis=0, tile...  17 us
    ppermute x1, starting transfers between devices, body(): partner = lax.ppermute(gathered[:, 1], 'mem', [(0, 1), (1, 0)])  3.53 us
    pallas_call x1, Pallas kernels, body(): pl.pallas_call(functools.partial(triple_kernel, sizes=sizes), out_shape=o...  3.32 us
    convert_element_type x3, local copies, waits for them, and re-layouts, body(): regrouped.reshape(1, lag_count, 2, tile_count, order).astype(jnp.float32)  2.83 us
    pallas_call x1, Pallas kernels, body(): pl.pallas_call(functools.partial(correlate_kernel, scale=2.0 / (2 * slot_...  2.7 us
    ppermute x1, waiting for transfers between devices, body(): partner = lax.ppermute(gathered[:, 1], 'mem', [(0, 1), (1, 0)])  2.36 us
  transfers between devices with their start and end apart: 1, of which 1 were waited for; matrix products, arithmetic and copies ran while one was open for 0% of the time, Pallas kernels for 1%

profile of v1, /device:TPU:8, one launch (start us, length us, event | category | flops | bytes accessed | tf_op | source)
XLA Modules:
  0.0 77.7 jit_solution(6140846417279844874)
XLA Ops:
  0.0 0.6 pad_add_fusion.place_ref
  0.6 3.3 %triple.1 = bf16[384,384]{1,0:T(8,128)(2,1)S(1)} custom-call(s32[2]{0:T(128)} %pad_add_fusion.place_ref, bf16[2,2,2,192,192]{4,3,2,1,0:T(8,128)(2,1)} %retarded_ref.1, bf16[1,2,2,192,192]{4,3,2,1,0:T(8,128)(2,1)} %self_energy_ref.1), custom_call_target="tpu_custom_call" | custom-call | tf_op jit(solution)/shard_map/triple/pallas_call | solution.py:149
  3.9 0.1 reshape.31
  4.0 42.8 %all_to_all.10 = bf16[192,2,384]{2,1,0:T(2,128)(2,1)S(1)} all-to-all(bf16[192,2,384]{2,1,0:T(2,128)(2,1)S(1)} %reshape.31), channel_id=1, replica_groups=mesh['pair'=2,'mem'=2,'tile'=24,'rep'=8] {'tile','rep'}, dimensions={0} | all-to-all | bytes 589824 | tf_op jit(solution)/shard_map/all_to_all | solution.py:165
  46.8 0.0 copy-start.4
  46.8 0.4 fusion
  47.2 0.0 copy-start.1
  47.3 3.5 %collective-permute-start = (bf16[192,384]{1,0:T(8,128)(2,1)S(1)}, bf16[192,384]{1,0:T(8,128)(2,1)S(1)}, u32[]{:S(2)}, u32[]{:S(2)}) collective-permute-start(bf16[192,384]{1,0:T(8,128)(2,1)S(1)} %bitcast.19), channel_id=1, source_target_pairs={{0,192},{192,0},{1,193},{193,1},{2,194},{194,2},{3,195},{195,3},{4... | collective-permute-start | bytes 442376 | tf_op jit(solution)/shard_map/ppermute | solution.py:166
  50.8 0.0 copy-done.4
  50.8 0.1 reshape.32
  51.0 0.1 copy.12
  51.1 0.0 copy-done.1
  51.1 0.0 copy-start.2
  51.1 0.0 copy-start.3
  51.1 0.8 %own_sums.1.own_ref = f32[768,256]{1,0:T(8,128)S(1)} custom-call(bf16[192,384]{1,0:T(8,128)(2,1)S(1)} %bitcast.15, s32[2,192]{1,0:T(2,128)S(1)} %bitcast.16, bf16[768,384]{1,0:T(8,128)(2,1)S(1)} %copy-done.1), custom_call_target="tpu_custom_call" | custom-call | tf_op jit(solution)/shard_map/own_sums/pallas_call | solution.py:176
  51.9 0.0 copy-start
  51.9 0.9 %copy-done = f32[768,256]{1,0:T(8,128)} copy-done((f32[768,256]{1,0:T(8,128)}, f32[768,256]{1,0:T(8,128)S(1)}, u32[]{:S(2)}) %copy-start) | copy-done | bytes 786456
  52.8 2.4 %collective-permute-done.signal_ref = bf16[192,384]{1,0:T(8,128)(2,1)S(1)} collective-permute-done((bf16[192,384]{1,0:T(8,128)(2,1)S(1)}, bf16[192,384]{1,0:T(8,128)(2,1)S(1)}, u32[]{:S(2)}, u32[]{:S(2)}) %collective-permute-start) | collective-permute-done | bytes 147488 | tf_op jit(solution)/shard_map/ppermute | solution.py:166
  55.2 0.0 copy-done.2
  55.2 0.0 copy-done.3
  55.2 2.7 %correlate.1 = bf16[2,192,384]{2,1,0:T(8,128)(2,1)S(1)} custom-call(f32[1]{0:T(128)} %bitcast.sign_ref, bf16[192,384]{1,0:T(8,128)(2,1)S(1)} %collective-permute-done.signal_ref, s32[2,192]{1,0:T(2,128)S(1)} %bitcast.17, bf16[768,384]{1,0:T(8,128)(2,1)S(1)} %copy-done.1, f32[768,256]{1,0:T(8,128)} %copy-done, bf16[384,384]{1,0:T(8,128)(2,1)S(1)} %copy-done.3, ...), custom_call_target="tpu_custom_call" | custom-call | tf_op jit(solution)/shard_map/correlate/pallas_call | solution.py:186
  57.9 17.0 %all_to_all.11 = bf16[48,8,384]{2,1,0:T(8,128)(2,1)S(1)} all-to-all(bf16[48,8,384]{2,1,0:T(8,128)(2,1)S(1)} %bitcast.14), channel_id=1, replica_groups=mesh['pair'=2,'mem'=2,'tile'=24,'rep'=8] {'mem','tile'}, dimensions={0} | all-to-all | bytes 589824 | tf_op jit(solution)/shard_map/all_to_all | solution.py:196
  74.9 0.9 %reshape.35 = f32[2,24,8,2,2,96]{5,4,3,2,1,0:T(2,128)S(1)} reshape(bf16[48,8,384]{2,1,0:T(8,128)(2,1)S(1)} %all_to_all.11) | data formatting | bytes 884736 | tf_op jit(solution)/shard_map/convert_element_type | solution.py:198
  75.7 0.6 copy.20
  76.4 1.3 %reshape.34 = f32[1,16,2,24,192]{4,3,2,1,0:T(8,128)} reshape(f32[2,8,2,24,2,96]{5,4,3,2,1,0:T(2,128)S(1)} %bitcast.18) | data formatting | bytes 1179648 | tf_op jit(solution)/shard_map/convert_element_type | solution.py:198
  (2 shorter events, 0.1 us)
Async XLA Ops:
  46.8 4.0 %copy-start.4 = (s32[384]{0:T(512)S(1)}, s32[384]{0:T(512)}, u32[]{:S(2)}) copy-start(s32[384]{0:T(512)} %param.8) | copy-start | bytes 4612
  47.2 3.9 %copy-start.1 = (bf16[768,384]{1,0:T(8,128)(2,1)S(1)}, bf16[768,384]{1,0:T(8,128)(2,1)}, u32[]{:S(2)}) copy-start(bf16[768,384]{1,0:T(8,128)(2,1)} %constant.18.clone.table_ref) | copy-start | bytes 1769476
  47.3 7.9 %collective-permute-start = (bf16[192,384]{1,0:T(8,128)(2,1)S(1)}, bf16[192,384]{1,0:T(8,128)(2,1)S(1)}, u32[]{:S(2)}, u32[]{:S(2)}) collective-permute-start(bf16[192,384]{1,0:T(8,128)(2,1)S(1)} %bitcast.19), channel_id=1, source_target_pairs={{0,192},{192,0},{1,193},{193,1},{2,194},{194,2},{3,195},{195,3},{4... | collective-permute-start | bytes 442376 | tf_op jit(solution)/shard_map/ppermute | solution.py:166
  51.1 4.1 %copy-start.2 = (bf16[384,384]{1,0:T(8,128)(2,1)S(1)}, bf16[384,384]{1,0:T(8,128)(2,1)}, u32[]{:S(2)}) copy-start(bf16[384,384]{1,0:T(8,128)(2,1)} %constant.20.clone.back_sin_ref) | copy-start | bytes 884740
  51.1 4.1 %copy-start.3 = (bf16[384,384]{1,0:T(8,128)(2,1)S(1)}, bf16[384,384]{1,0:T(8,128)(2,1)}, u32[]{:S(2)}) copy-start(bf16[384,384]{1,0:T(8,128)(2,1)} %constant.19.clone.back_cos_ref) | copy-start | bytes 884740
  51.9 0.9 %copy-start = (f32[768,256]{1,0:T(8,128)}, f32[768,256]{1,0:T(8,128)S(1)}, u32[]{:S(2)}) copy-start(f32[768,256]{1,0:T(8,128)S(1)} %own_sums.1.own_ref) | copy-start | bytes 2359300

commit v2 on v1

v2 whole, which is shorter than its diff:
```python
import functools
import math

import jax
import jax.numpy as jnp
import numpy as np
from jax import lax
from jax.experimental import pallas as pl
from jax.experimental.pallas import tpu as pltpu
from jax.sharding import Mesh, PartitionSpec as P

LANES = 128
INTERPRET = False


def twiddles(count):
    steps = (2 * np.arange(count)[:, None] + 1) * np.arange(count)[None, :] % (4 * count)
    angles = steps * (math.pi / (2 * count))
    return np.cos(angles), np.sin(angles)


def dot(left_side, right_side):
    return jnp.dot(left_side, right_side, preferred_element_type=jnp.float32)


def dot_rows(left_side, right_side):
    return lax.dot_general(left_side, right_side, (((1,), (1,)), ((), ())), preferred_element_type=jnp.float32)


def one_hot(condition):
    return jnp.where(condition, 1.0, 0.0).astype(jnp.bfloat16)


def triple_kernel(retarded_ref, self_energy_ref, own_ref, away_ref, green_ref, sigma_ref, left_ref, right_ref, sems, *, sizes):
    tile_count, hop_count = sizes
    energies, _, order, _ = green_ref.shape
    half = order // 2
    momentum, member, core = lax.axis_index("pair"), lax.axis_index("mem"), lax.axis_index("core")
    copies = []
    for e in range(energies):
        pair = (
            pltpu.make_async_copy(retarded_ref.at[momentum, e], green_ref.at[e], sems.at[e, 0]),
            pltpu.make_async_copy(self_energy_ref.at[0, e], sigma_ref.at[e], sems.at[e, 1]),
        )
        for copy in pair:
            copy.start()
        copies.append(pair)
    target = lax.broadcasted_iota(jnp.int32, (order, order), 0)
    source = lax.broadcasted_iota(jnp.int32, (order, order), 1)
    away = jnp.where(target >= half, 1, 0)
    device = target - away * half
    to_core = core + away - 2 * core * away
    row = (2 * (device & (hop_count - 1)) + to_core) * tile_count + (device >> (hop_count.bit_length() - 1))
    pick = one_hot(source == row)
    sums = []
    for e in range(energies):
        for copy in copies[e]:
            copy.wait()
        green_re, green_im = green_ref[e, 0], green_ref[e, 1]
        sigma_re, sigma_im = sigma_ref[e, 0], sigma_ref[e, 1]
        cross_re = (dot(green_re, sigma_re) - dot(green_im, sigma_im)).astype(jnp.bfloat16)
        cross_im = (dot(green_re, sigma_im) + dot(green_im, sigma_re)).astype(jnp.bfloat16)

        def set_sides(left_re, left_im, right_re, right_im, conj):
            left_ref[0], left_ref[1] = left_re, left_im
            for side in range(2):
                re, im = right_re[side * half : (side + 1) * half], right_im[side * half : (side + 1) * half]
                right_ref[side, 0, :half], right_ref[side, 0, half:] = re, -im if conj else im
                right_ref[side, 1, :half], right_ref[side, 1, half:] = im, re if conj else -re

        @pl.when(member == 0)
        def _():
            set_sides(cross_re, cross_im, green_re, green_im, True)

        @pl.when(member == 1)
        def _():
            set_sides(green_re, green_im, cross_re, cross_im, False)

        left = [dot(pick, left_ref[part]).astype(jnp.bfloat16) for part in range(2)]
        sums.append(
            [dot_rows(left[0], right_ref[side, 0]) + dot_rows(left[1], right_ref[side, 1]) for side in range(2)]
        )
    for start, out_ref in ((0, own_ref), (half, away_ref)):
        for side in range(2):
            out_ref[side * half : (side + 1) * half] = jnp.concatenate(
                [sums[e][side][start : start + half] for e in range(energies)], axis=1
            ).astype(jnp.bfloat16)


def times(left, right):
    left_re, left_im = left[:, :LANES], left[:, LANES:]
    right_re, right_im = right[:, :LANES], right[:, LANES:]
    return left_re * right_re - left_im * right_im, left_re * right_im + left_im * right_re


def correlate_kernel(signal_ref, energy_ref, table_ref, back_cos_ref, back_sin_ref, out_ref, ordered_ref, *, scale):
    energies, devices = energy_ref.shape
    count = energies * devices
    half = signal_ref.shape[1] // (2 * energies)
    grid_index = lax.broadcasted_iota(jnp.int32, (count, devices), 0)
    picks = [one_hot(grid_index == energy_ref[e : e + 1]) for e in range(energies)]
    ordered_ref[...] = jnp.zeros(ordered_ref.shape, ordered_ref.dtype)
    for component in range(2):
        signal = signal_ref[component * devices : (component + 1) * devices]
        for part in range(2):
            total = None
            for e in range(energies):
                start = (2 * e + part) * half
                term = dot(picks[e], signal[:, start : start + half])
                total = term if total is None else total + term
            lane = (2 * component + part) * LANES
            ordered_ref[:, lane : lane + half] = total.astype(jnp.bfloat16)
    one_cos, one_sin = (dot(table_ref[r * count : (r + 1) * count], ordered_ref[:, : 2 * LANES]) for r in range(2))
    two_cos, two_sin = (dot(table_ref[r * count : (r + 1) * count], ordered_ref[:, 2 * LANES :]) for r in range(2))
    even_parts = [a + b for a, b in zip(times(one_cos, two_cos), times(one_sin, two_sin))]
    odd_parts = [a - b for a, b in zip(times(one_sin, two_cos), times(one_cos, two_sin))]
    even = dot(back_cos_ref[...], jnp.concatenate(even_parts, axis=1).astype(jnp.bfloat16))
    odd = dot(back_sin_ref[...], jnp.concatenate(odd_parts, axis=1).astype(jnp.bfloat16))
    rows = count // 2
    for component, total in enumerate((even + odd, even - odd)):
        re = total[:, LANES : LANES + half] * scale
        im = total[:, :half] * -scale
        out_ref[component] = jnp.concatenate([re[:rows], im[:rows], re[rows:], im[rows:]], axis=1).astype(out_ref.dtype)


def on_chip(array):
    return pltpu.with_memory_space_constraint(array, pltpu.VMEM) if not INTERPRET else array


def on_chip_out(shape, dtype):
    return pltpu.VMEM(shape, dtype) if not INTERPRET else jax.ShapeDtypeStruct(shape, dtype)


def body(retarded, self_energy, energy_of, *, sizes):
    tile_count, hop_count = sizes
    energies, order = retarded.shape[1], retarded.shape[3]
    half = order // 2
    slot_count = energy_of.shape[0]
    in_vmem = pl.BlockSpec(memory_space=pltpu.VMEM)
    in_place = pl.BlockSpec(memory_space=pl.ANY)
    block = on_chip_out((order, 2 * energies * half), jnp.bfloat16)
    own, away = pl.pallas_call(
        functools.partial(triple_kernel, sizes=sizes),
        out_shape=(block, block),
        in_specs=[in_place, in_place],
        out_specs=(in_vmem, in_vmem),
        scratch_shapes=[
            pltpu.VMEM((energies, 2, order, order), jnp.bfloat16),
            pltpu.VMEM((energies, 2, order, order), jnp.bfloat16),
            pltpu.VMEM((2, order, order), jnp.bfloat16),
            pltpu.VMEM((2, 2, order, order), jnp.bfloat16),
            pltpu.SemaphoreType.DMA((energies, 2)),
        ],
        interpret=INTERPRET,
        name="triple",
    )(retarded, self_energy)
    sibling = lax.ppermute(away, "core", [(0, 1), (1, 0)])
    by_core = energy_of.reshape(slot_count // (2 * energies), 2, energies)
    by_core = jnp.where(lax.axis_index("core") == 0, by_core, by_core[:, ::-1])
    energy = by_core.reshape(slot_count // energies, energies).T
    blocks, energy = lax.optimization_barrier((jnp.stack([own, sibling], axis=1), energy))
    gathered = lax.all_to_all(blocks, ("mem", "tile", "zh"), split_axis=0, concat_axis=0, tiled=True)

    cos_part, sin_part = twiddles(slot_count)
    table = on_chip(jnp.asarray(np.concatenate([cos_part, sin_part]), jnp.bfloat16))
    lag_count = slot_count // tile_count
    lags = np.arange(slot_count).reshape(tile_count, 2, lag_count // 2).transpose(1, 0, 2).reshape(-1)
    back_cos = on_chip(jnp.asarray(cos_part.T[lags], jnp.bfloat16))
    back_sin = on_chip(jnp.asarray(sin_part.T[lags], jnp.bfloat16))
    polar = pl.pallas_call(
        functools.partial(correlate_kernel, scale=2.0 / (2 * slot_count * math.sqrt(slot_count))),
        out_shape=on_chip_out((2, slot_count // 2, 4 * half), jnp.bfloat16),
        in_specs=[in_vmem] * 5,
        out_specs=in_vmem,
        scratch_shapes=[pltpu.VMEM((slot_count, 4 * LANES), jnp.bfloat16)],
        interpret=INTERPRET,
        name="correlate",
    )(on_chip(gathered.reshape(2 * order, 2 * energies * half)), on_chip(energy), table, back_cos, back_sin)
    packed = polar.reshape(2 * tile_count, lag_count // 2, 4 * half)
    regrouped = lax.all_to_all(packed, ("mem", "tile"), split_axis=0, concat_axis=0, tiled=True)
    regrouped = regrouped.reshape(2, tile_count, lag_count // 2, 2, 2, half).transpose(3, 2, 4, 1, 0, 5)
    return regrouped.reshape(1, lag_count, 2, tile_count, order).astype(jnp.float32)


def solution(mesh):
    comp, tile, rep = mesh.devices.shape
    split = Mesh(mesh.devices.reshape(2, comp // 2, tile, rep // 2, 2), ("pair", "mem", "tile", "zh", "core"))
    energy_axes = ("tile", "zh", "core")
    placed = (
        P(None, energy_axes, None, None, None),
        P(("pair", "mem"), energy_axes, None, None, None),
        P(),
    )
    return jax.shard_map(
        functools.partial(body, sizes=(tile, rep // 2)),
        mesh=split,
        in_specs=placed,
        out_specs=P(("pair", "mem"), "tile", None, ("zh", "core"), None),
        check_vma=False,
    )
```

time: 78 us -> 72.8 us (0.933)
  Pallas kernels: 6.82 us -> 4.23 us
  waiting for transfers between devices: 2.36 us -> 0.14 us
  starting transfers between devices: 3.53 us -> 1.92 us
  blocking collectives: 59.8 us -> 60.7 us
  local copies, waits for them, and re-layouts: 4.52 us -> 5.33 us
    ppermute x1, waiting for transfers between devices: 2.36 us -> 0.14 us  [body(): sibling = lax.ppermute(away, 'core', [(0, 1), (1, 0)])]
    ppermute x1, starting transfers between devices: 3.53 us -> 1.92 us  [body(): sibling = lax.ppermute(away, 'core', [(0, 1), (1, 0)])]
    all_to_all x1, blocking collectives: 42.8 us -> 44.3 us  [body(): lax.all_to_all(blocks, ('mem', 'tile', 'zh'), split_axis=0, concat_axis=0...]
    pallas_call x2 -> x1, Pallas kernels: 4.12 us -> 2.69 us  [body(): pl.pallas_call(functools.partial(triple_kernel, sizes=sizes), out_shape=(...]
    pallas_call x1, Pallas kernels: 2.7 us -> 1.53 us  [body(): pl.pallas_call(functools.partial(correlate_kernel, scale=2.0 / (2 * slot_...]
    unnamed x12 -> x8, local copies, waits for them, and re-layouts: 0.95 us -> 1.61 us
  transfers between devices with their start and end apart: 1 -> 1, of which waited for: 1 -> 1; matrix products, arithmetic and copies ran while one was open for 0% -> 1% of each run, Pallas kernels for 1% -> 0%
where the time goes in v2:
time: 72.8 us; the launch traced here: 72.5 us
  blocking collectives  60.7 us (83%)
  local copies, waits for them, and re-layouts  5.33 us (7%)
  Pallas kernels  4.23 us (6%)
  starting transfers between devices  1.92 us (3%)
    all_to_all x1, blocking collectives, body(): lax.all_to_all(blocks, ('mem', 'tile', 'zh'), split_axis=0, concat_axis=0...  44.3 us
    all_to_all x1, blocking collectives, body(): lax.all_to_all(packed, ('mem', 'tile'), split_axis=0, concat_axis=0, tile...  16.4 us
    convert_element_type x3, local copies, waits for them, and re-layouts, body(): regrouped.reshape(1, lag_count, 2, tile_count, order).astype(jnp.float32)  2.83 us
    pallas_call x1, Pallas kernels, body(): pl.pallas_call(functools.partial(triple_kernel, sizes=sizes), out_shape=(...  2.69 us
    ppermute x1, starting transfers between devices, body(): sibling = lax.ppermute(away, 'core', [(0, 1), (1, 0)])  1.92 us
    unnamed x8, local copies, waits for them, and re-layouts  1.61 us
    pallas_call x1, Pallas kernels, body(): pl.pallas_call(functools.partial(correlate_kernel, scale=2.0 / (2 * slot_...  1.53 us
  transfers between devices with their start and end apart: 1, of which 1 were waited for; matrix products, arithmetic and copies ran while one was open for 1% of the time, Pallas kernels for 0%

profile of v2, /device:TPU:8, one launch (start us, length us, event | category | flops | bytes accessed | tf_op | source)
XLA Modules:
  0.0 72.5 jit_solution(12610972634836620819)
XLA Ops:
  0.0 2.7 %triple.1 = (bf16[192,384]{1,0:T(8,128)(2,1)S(1)}, bf16[192,384]{1,0:T(8,128)(2,1)S(1)}) custom-call(bf16[2,2,2,192,192]{4,3,2,1,0:T(8,128)(2,1)} %retarded_ref.1, bf16[1,2,2,192,192]{4,3,2,1,0:T(8,128)(2,1)} %self_energy_ref.1), custom_call_target="tpu_custom_call" | custom-call | tf_op jit(solution)/shard_map/triple/pallas_call | solution.py:142
  2.7 1.9 %collective-permute-start = (bf16[192,384]{1,0:T(8,128)(2,1)S(1)}, bf16[192,384]{1,0:T(8,128)(2,1)S(1)}, u32[]{:S(2)}, u32[]{:S(2)}) collective-permute-start(bf16[192,384]{1,0:T(8,128)(2,1)S(1)} %get-tuple-element.10), channel_id=1, source_target_pairs={{0,1},{1,0},{2,3},{3,2},{4,5},{5,4},{6,7},{7,6},{8,9},{9,8},{10,11... | collective-permute-start | bytes 442376 | tf_op jit(solution)/shard_map/ppermute | solution.py:157
  4.6 0.0 copy-start.3
  4.6 0.7 copy-done.3
  5.3 0.2 reshape.30
  5.5 0.2 rev.3
  5.8 0.1 copy.15
  5.8 0.1 collective-permute-done
  6.0 0.3 copy.13
  6.3 0.0 copy-start
  6.3 44.3 %all_to_all.10 = bf16[192,2,384]{2,1,0:T(2,128)(2,1)S(1)} all-to-all(bf16[192,2,384]{2,1,0:T(2,128)(2,1)S(1)} %copy.13), channel_id=1, replica_groups=mesh['pair'=2,'mem'=2,'tile'=24,'zh'=4,'core'=2] {'mem','tile','zh'}, dimensions={0} | all-to-all | bytes 589824 | tf_op jit(solution)/shard_map/all_to_all | solution.py:162
  50.7 0.0 copy-start.1
  50.7 0.0 copy-start.2
  50.7 0.1 reshape.32.signal_ref
  50.8 0.0 copy-done
  50.8 0.8 %copy-done.1 = bf16[384,384]{1,0:T(8,128)(2,1)S(1)} copy-done((bf16[384,384]{1,0:T(8,128)(2,1)S(1)}, bf16[384,384]{1,0:T(8,128)(2,1)}, u32[]{:S(2)}) %copy-start.1) | copy-done | bytes 294936
  51.6 0.1 copy-done.2
  51.7 1.5 %correlate.1 = bf16[2,192,384]{2,1,0:T(8,128)(2,1)S(1)} custom-call(bf16[384,384]{1,0:T(8,128)(2,1)S(1)} %reshape.32.signal_ref, s32[2,192]{1,0:T(2,128)S(1)} %bitcast.13, bf16[768,384]{1,0:T(8,128)(2,1)S(1)} %copy-done, bf16[384,384]{1,0:T(8,128)(2,1)S(1)} %copy-done.2, bf16[384,384]{1,0:T(8,128)(2,1)S(1)} %copy-done.1), custom_call_target="tpu_custom_call" | custom-call | tf_op jit(solution)/shard_map/correlate/pallas_call | solution.py:170
  53.3 16.4 %all_to_all.11 = bf16[48,8,384]{2,1,0:T(8,128)(2,1)S(1)} all-to-all(bf16[48,8,384]{2,1,0:T(8,128)(2,1)S(1)} %bitcast.11), channel_id=1, replica_groups=mesh['pair'=2,'mem'=2,'tile'=24,'zh'=4,'core'=2] {'mem','tile'}, dimensions={0} | all-to-all | bytes 589824 | tf_op jit(solution)/shard_map/all_to_all | solution.py:180
  69.6 0.9 %reshape.35 = f32[2,24,8,2,2,96]{5,4,3,2,1,0:T(2,128)S(1)} reshape(bf16[48,8,384]{2,1,0:T(8,128)(2,1)S(1)} %all_to_all.11) | data formatting | bytes 884736 | tf_op jit(solution)/shard_map/convert_element_type | solution.py:182
  70.5 0.6 copy.17
  71.1 1.3 %reshape.34 = f32[1,16,2,24,192]{4,3,2,1,0:T(8,128)} reshape(f32[2,8,2,24,2,96]{5,4,3,2,1,0:T(2,128)S(1)} %bitcast.14) | data formatting | bytes 1179648 | tf_op jit(solution)/shard_map/convert_element_type | solution.py:182
  (2 shorter events, 0.1 us)
Async XLA Ops:
  2.7 3.3 %collective-permute-start = (bf16[192,384]{1,0:T(8,128)(2,1)S(1)}, bf16[192,384]{1,0:T(8,128)(2,1)S(1)}, u32[]{:S(2)}, u32[]{:S(2)}) collective-permute-start(bf16[192,384]{1,0:T(8,128)(2,1)S(1)} %get-tuple-element.10), channel_id=1, source_target_pairs={{0,1},{1,0},{2,3},{3,2},{4,5},{5,4},{6,7},{7,6},{8,9},{9,8},{10,11... | collective-permute-start | bytes 442376 | tf_op jit(solution)/shard_map/ppermute | solution.py:157
  4.6 0.7 copy-start.3
  6.3 44.5 %copy-start = (bf16[768,384]{1,0:T(8,128)(2,1)S(1)}, bf16[768,384]{1,0:T(8,128)(2,1)}, u32[]{:S(2)}) copy-start(bf16[768,384]{1,0:T(8,128)(2,1)} %constant.12.clone.table_ref) | copy-start | bytes 1769476
  50.7 1.0 %copy-start.1 = (bf16[384,384]{1,0:T(8,128)(2,1)S(1)}, bf16[384,384]{1,0:T(8,128)(2,1)}, u32[]{:S(2)}) copy-start(bf16[384,384]{1,0:T(8,128)(2,1)} %constant.14.clone.back_sin_ref) | copy-start | bytes 884740
  50.7 1.0 %copy-start.2 = (bf16[384,384]{1,0:T(8,128)(2,1)S(1)}, bf16[384,384]{1,0:T(8,128)(2,1)}, u32[]{:S(2)}) copy-start(bf16[384,384]{1,0:T(8,128)(2,1)} %constant.13.clone.back_cos_ref) | copy-start | bytes 884740

commit v3 on v2

--- a/solution.py
+++ b/solution.py
@@ -31,7 +31,10 @@
     return jnp.where(condition, 1.0, 0.0).astype(jnp.bfloat16)
 
 
-def triple_kernel(retarded_ref, self_energy_ref, own_ref, away_ref, green_ref, sigma_ref, left_ref, right_ref, sems, *, sizes):
+def triple_kernel(
+    retarded_ref, self_energy_ref, energy_ref, table_ref, own_ref, away_ref, energy_out_ref, table_out_ref,
+    green_ref, sigma_ref, left_ref, right_ref, sems, *, sizes
+):
     tile_count, hop_count = sizes
     energies, _, order, _ = green_ref.shape
     half = order // 2
@@ -45,6 +48,14 @@
         for copy in pair:
             copy.start()
         copies.append(pair)
+    copies.append(
+        (
+            pltpu.make_async_copy(energy_ref, energy_out_ref, sems.at[energies, 0]),
+            pltpu.make_async_copy(table_ref, table_out_ref, sems.at[energies, 1]),
+        )
+    )
+    for copy in copies[energies]:
+        copy.start()
     target = lax.broadcasted_iota(jnp.int32, (order, order), 0)
     source = lax.broadcasted_iota(jnp.int32, (order, order), 1)
     away = jnp.where(target >= half, 1, 0)
@@ -85,6 +96,23 @@
             out_ref[side * half : (side + 1) * half] = jnp.concatenate(
                 [sums[e][side][start : start + half] for e in range(energies)], axis=1
             ).astype(jnp.bfloat16)
+    for copy in copies[energies]:
+        copy.wait()
+
+
+def pick_kernel(energy_ref, out_ref):
+    energies, count, devices = out_ref.shape
+    core = lax.axis_index("core")
+    slots = jnp.concatenate([energy_ref[r : r + 1] for r in range(energy_ref.shape[0])], axis=1)
+    digit = lax.broadcasted_iota(jnp.int32, (16, count), 0)
+    digits = jnp.where(digit == 0, slots >> 1, slots & 1).astype(jnp.float32).astype(jnp.bfloat16)
+    slot = lax.broadcasted_iota(jnp.int32, (count, devices), 0)
+    device = lax.broadcasted_iota(jnp.int32, (count, devices), 1)
+    side = device & 1
+    first = ((device >> 1) * 2 + side + core - 2 * side * core) * energies
+    for e in range(energies):
+        taken = dot(digits, one_hot(slot == first + e))
+        out_ref[e] = one_hot(slot == (2.0 * taken[:1] + taken[1:2]).astype(jnp.int32))
 
 
 def times(left, right):
@@ -93,34 +121,55 @@
     return left_re * right_re - left_im * right_im, left_re * right_im + left_im * right_re
 
 
-def correlate_kernel(signal_ref, energy_ref, table_ref, back_cos_ref, back_sin_ref, out_ref, ordered_ref, *, scale):
-    energies, devices = energy_ref.shape
-    count = energies * devices
+def correlate_kernel(signal_ref, pick_ref, table_ref, out_ref, *, scale):
+    energies, count, devices = pick_ref.shape
     half = signal_ref.shape[1] // (2 * energies)
-    grid_index = lax.broadcasted_iota(jnp.int32, (count, devices), 0)
-    picks = [one_hot(grid_index == energy_ref[e : e + 1]) for e in range(energies)]
-    ordered_ref[...] = jnp.zeros(ordered_ref.shape, ordered_ref.dtype)
+    gap = jnp.zeros((devices, LANES - half), jnp.bfloat16)
+    sums = []
     for component in range(2):
         signal = signal_ref[component * devices : (component + 1) * devices]
-        for part in range(2):
-            total = None
-            for e in range(energies):
-                start = (2 * e + part) * half
-                term = dot(picks[e], signal[:, start : start + half])
-                total = term if total is None else total + term
-            lane = (2 * component + part) * LANES
-            ordered_ref[:, lane : lane + half] = total.astype(jnp.bfloat16)
-    one_cos, one_sin = (dot(table_ref[r * count : (r + 1) * count], ordered_ref[:, : 2 * LANES]) for r in range(2))
-    two_cos, two_sin = (dot(table_ref[r * count : (r + 1) * count], ordered_ref[:, 2 * LANES :]) for r in range(2))
+        ordered = None
+        for e in range(energies):
+            re, im = (signal[:, (2 * e + part) * half : (2 * e + part + 1) * half] for part in range(2))
+            term = dot(pick_ref[e], jnp.concatenate([re, gap, im, gap], axis=1))
+            ordered = term if ordered is None else ordered + term
+        ordered = ordered.astype(jnp.bfloat16)
+        sums.append([dot(table_ref[r * count : (r + 1) * count], ordered) for r in range(2)])
+    (one_cos, one_sin), (two_cos, two_sin) = sums
     even_parts = [a + b for a, b in zip(times(one_cos, two_cos), times(one_sin, two_sin))]
     odd_parts = [a - b for a, b in zip(times(one_sin, two_cos), times(one_cos, two_sin))]
-    even = dot(back_cos_ref[...], jnp.concatenate(even_parts, axis=1).astype(jnp.bfloat16))
-    odd = dot(back_sin_ref[...], jnp.concatenate(odd_parts, axis=1).astype(jnp.bfloat16))
+    even = dot(table_ref[2 * count : 3 * count], jnp.concatenate(even_parts, axis=1).astype(jnp.bfloat16))
+    odd = dot(table_ref[3 * count :], jnp.concatenate(odd_parts, axis=1).astype(jnp.bfloat16))
     rows = count // 2
     for component, total in enumerate((even + odd, even - odd)):
         re = total[:, LANES : LANES + half] * scale
         im = total[:, :half] * -scale
         out_ref[component] = jnp.concatenate([re[:rows], im[:rows], re[rows:], im[rows:]], axis=1).astype(out_ref.dtype)
+
+
+def place_kernel(gathered_ref, out_ref, placed_ref, sems):
+    _, lags, _, tiles, order = out_ref.shape
+    half, low = order // 2, lags // 2
+    rows = low * tiles
+    target = lax.broadcasted_iota(jnp.int32, (rows, rows), 0)
+    source = lax.broadcasted_iota(jnp.int32, (rows, rows), 1)
+    pick = one_hot((source & (low - 1)) * tiles + (source >> (low.bit_length() - 1)) == target)
+    copies = []
+    for high in range(2):
+        for part in range(2):
+            lane = (2 * high + part) * half
+            both = [gathered_ref[side * rows : (side + 1) * rows, lane : lane + half] for side in range(2)]
+            moved = dot(pick, jnp.concatenate(both, axis=1))
+            for lag in range(low):
+                placed_ref[high, part, lag] = moved[lag * tiles : (lag + 1) * tiles]
+            copies.append(
+                pltpu.make_async_copy(
+                    placed_ref.at[high, part], out_ref.at[0, pl.ds(high * low, low), part], sems.at[high, part]
+                )
+            )
+            copies[-1].start()
+    for copy in copies:
+        copy.wait()
 
 
 def on_chip(array):
@@ -138,48 +187,61 @@
     slot_count = energy_of.shape[0]
     in_vmem = pl.BlockSpec(memory_space=pltpu.VMEM)
     in_place = pl.BlockSpec(memory_space=pl.ANY)
+    cos_part, sin_part = twiddles(slot_count)
+    lag_count = slot_count // tile_count
+    lags = np.arange(slot_count).reshape(tile_count, 2, lag_count // 2).transpose(1, 0, 2).reshape(-1)
+    table = jnp.asarray(np.concatenate([cos_part, sin_part, cos_part.T[lags], sin_part.T[lags]]), jnp.bfloat16)
+    lanes = math.gcd(slot_count, LANES)
+    slot_energy = energy_of.reshape(slot_count // lanes, lanes)
     block = on_chip_out((order, 2 * energies * half), jnp.bfloat16)
-    own, away = pl.pallas_call(
+    own, away, slot_energy, table = pl.pallas_call(
         functools.partial(triple_kernel, sizes=sizes),
-        out_shape=(block, block),
-        in_specs=[in_place, in_place],
-        out_specs=(in_vmem, in_vmem),
+        out_shape=(block, block, on_chip_out(slot_energy.shape, jnp.int32), on_chip_out(table.shape, jnp.bfloat16)),
+        in_specs=[in_place] * 4,
+        out_specs=(in_vmem,) * 4,
         scratch_shapes=[
             pltpu.VMEM((energies, 2, order, order), jnp.bfloat16),
             pltpu.VMEM((energies, 2, order, order), jnp.bfloat16),
             pltpu.VMEM((2, order, order), jnp.bfloat16),
             pltpu.VMEM((2, 2, order, order), jnp.bfloat16),
-            pltpu.SemaphoreType.DMA((energies, 2)),
+            pltpu.SemaphoreType.DMA((energies + 1, 2)),
         ],
         interpret=INTERPRET,
         name="triple",
-    )(retarded, self_energy)
+    )(retarded, self_energy, slot_energy, table)
     sibling = lax.ppermute(away, "core", [(0, 1), (1, 0)])
-    by_core = energy_of.reshape(slot_count // (2 * energies), 2, energies)
-    by_core = jnp.where(lax.axis_index("core") == 0, by_core, by_core[:, ::-1])
-    energy = by_core.reshape(slot_count // energies, energies).T
-    blocks, energy = lax.optimization_barrier((jnp.stack([own, sibling], axis=1), energy))
+    picks = pl.pallas_call(
+        pick_kernel,
+        out_shape=on_chip_out((energies, slot_count, slot_count // energies), jnp.bfloat16),
+        in_specs=[in_vmem],
+        out_specs=in_vmem,
+        interpret=INTERPRET,
+        name="picks",
+    )(on_chip(slot_energy))
+    blocks, picks = lax.optimization_barrier((jnp.stack([own, sibling], axis=1), picks))
     gathered = lax.all_to_all(blocks, ("mem", "tile", "zh"), split_axis=0, concat_axis=0, tiled=True)
-
-    cos_part, sin_part = twiddles(slot_count)
-    table = on_chip(jnp.asarray(np.concatenate([cos_part, sin_part]), jnp.bfloat16))
-    lag_count = slot_count // tile_count
-    lags = np.arange(slot_count).reshape(tile_count, 2, lag_count // 2).transpose(1, 0, 2).reshape(-1)
-    back_cos = on_chip(jnp.asarray(cos_part.T[lags], jnp.bfloat16))
-    back_sin = on_chip(jnp.asarray(sin_part.T[lags], jnp.bfloat16))
     polar = pl.pallas_call(
         functools.partial(correlate_kernel, scale=2.0 / (2 * slot_count * math.sqrt(slot_count))),
         out_shape=on_chip_out((2, slot_count // 2, 4 * half), jnp.bfloat16),
-        in_specs=[in_vmem] * 5,
+        in_specs=[in_vmem] * 3,
         out_specs=in_vmem,
-        scratch_shapes=[pltpu.VMEM((slot_count, 4 * LANES), jnp.bfloat16)],
         interpret=INTERPRET,
         name="correlate",
-    )(on_chip(gathered.reshape(2 * order, 2 * energies * half)), on_chip(energy), table, back_cos, back_sin)
+    )(on_chip(gathered.reshape(2 * order, 2 * energies * half)), on_chip(picks), on_chip(table))
     packed = polar.reshape(2 * tile_count, lag_count // 2, 4 * half)
     regrouped = lax.all_to_all(packed, ("mem", "tile"), split_axis=0, concat_axis=0, tiled=True)
-    regrouped = regrouped.reshape(2, tile_count, lag_count // 2, 2, 2, half).transpose(3, 2, 4, 1, 0, 5)
-    return regrouped.reshape(1, lag_count, 2, tile_count, order).astype(jnp.float32)
+    return pl.pallas_call(
+        place_kernel,
+        out_shape=jax.ShapeDtypeStruct((1, lag_count, 2, tile_count, order), jnp.float32),
+        in_specs=[in_vmem],
+        out_specs=in_place,
+        scratch_shapes=[
+            pltpu.VMEM((2, 2, lag_count // 2, tile_count, order), jnp.float32),
+            pltpu.SemaphoreType.DMA((2, 2)),
+        ],
+        interpret=INTERPRET,
+        name="place",
+    )(on_chip(regrouped.reshape(tile_count * lag_count, 4 * half)))
 
 
 def solution(mesh):

time: 72.8 us -> 69.8 us (0.959)
  the two profiles are of different devices: /device:TPU:8 before, /device:TPU:4 now
where the time goes in v3:
time: 69.8 us; the launch traced here: 69.6 us
  blocking collectives  60.2 us (86%)
  Pallas kernels  5.93 us (8%)
  starting transfers between devices  1.92 us (3%)
  waiting for transfers between devices  1 us (1%)
    all_to_all x1, blocking collectives, body(): lax.all_to_all(blocks, ('mem', 'tile', 'zh'), split_axis=0, concat_axis=0...  44.3 us
    all_to_all x1, blocking collectives, body(): lax.all_to_all(packed, ('mem', 'tile'), split_axis=0, concat_axis=0, tile...  15.9 us
    pallas_call x1, Pallas kernels, body(): pl.pallas_call(functools.partial(triple_kernel, sizes=sizes), out_shape=(...  2.71 us
    ppermute x1, starting transfers between devices, body(): sibling = lax.ppermute(away, 'core', [(0, 1), (1, 0)])  1.92 us
    pallas_call x1, Pallas kernels, body(): pl.pallas_call(functools.partial(correlate_kernel, scale=2.0 / (2 * slot_...  1.69 us
  transfers between devices with their start and end apart: 1, of which 1 were waited for; matrix products, arithmetic and copies ran while one was open for 0% of the time, Pallas kernels for 0%

profile of v3, /device:TPU:4, one launch (start us, length us, event | category | flops | bytes accessed | tf_op | source)
XLA Modules:
  0.0 69.6 jit_solution(13778464755552818737)
XLA Ops:
  0.0 2.7 %triple.1 = (bf16[192,384]{1,0:T(8,128)(2,1)S(1)}, bf16[192,384]{1,0:T(8,128)(2,1)S(1)}, s32[3,128]{1,0:T(4,128)S(1)}, bf16[1536,384]{1,0:T(8,128)(2,1)S(1)}) custom-call(bf16[2,2,2,192,192]{4,3,2,1,0:T(8,128)(2,1)} %retarded_ref.1, bf16[1,2,2,192,192]{4,3,2,1,0:T(8,128)(2,1)} %self_energy_ref.1, s32[3,128]{1,0:T(4,128)} %bitcast.9, ...), custom_call_target="tpu_custom_call" | custom-call | tf_op jit(solution)/shard_map/triple/pallas_call | solution.py:197
  2.7 1.9 %collective-permute-start = (bf16[192,384]{1,0:T(8,128)(2,1)S(1)}, bf16[192,384]{1,0:T(8,128)(2,1)S(1)}, u32[]{:S(2)}, u32[]{:S(2)}) collective-permute-start(bf16[192,384]{1,0:T(8,128)(2,1)S(1)} %get-tuple-element.12), channel_id=1, source_target_pairs={{0,1},{1,0},{2,3},{3,2},{4,5},{5,4},{6,7},{7,6},{8,9},{9,8},{10,11... | collective-permute-start | bytes 442376 | tf_op jit(solution)/shard_map/ppermute | solution.py:212
  4.7 0.3 picks.1.pick_ref
  5.0 1.0 %collective-permute-done = bf16[192,384]{1,0:T(8,128)(2,1)S(1)} collective-permute-done((bf16[192,384]{1,0:T(8,128)(2,1)S(1)}, bf16[192,384]{1,0:T(8,128)(2,1)S(1)}, u32[]{:S(2)}, u32[]{:S(2)}) %collective-permute-start) | collective-permute-done | bytes 147488 | tf_op jit(solution)/shard_map/ppermute | solution.py:212
  6.0 0.3 copy.6
  6.3 44.3 %all_to_all.10 = bf16[192,2,384]{2,1,0:T(2,128)(2,1)S(1)} all-to-all(bf16[192,2,384]{2,1,0:T(2,128)(2,1)S(1)} %copy.6), channel_id=1, replica_groups=mesh['pair'=2,'mem'=2,'tile'=24,'zh'=4,'core'=2] {'mem','tile','zh'}, dimensions={0} | all-to-all | bytes 589824 | tf_op jit(solution)/shard_map/all_to_all | solution.py:222
  50.7 0.1 reshape.13.signal_ref
  50.8 1.7 %correlate.1 = bf16[2,192,384]{2,1,0:T(8,128)(2,1)S(1)} custom-call(bf16[384,384]{1,0:T(8,128)(2,1)S(1)} %reshape.13.signal_ref, bf16[2,384,192]{2,1,0:T(8,128)(2,1)S(1)} %picks.1.pick_ref, bf16[1536,384]{1,0:T(8,128)(2,1)S(1)} %get-tuple-element.16.table_ref), custom_call_target="tpu_custom_call" | custom-call | tf_op jit(solution)/shard_map/correlate/pallas_call | solution.py:223
  52.5 15.9 %all_to_all.11 = bf16[48,8,384]{2,1,0:T(8,128)(2,1)S(1)} all-to-all(bf16[48,8,384]{2,1,0:T(8,128)(2,1)S(1)} %bitcast.5), channel_id=1, replica_groups=mesh['pair'=2,'mem'=2,'tile'=24,'zh'=4,'core'=2] {'mem','tile'}, dimensions={0} | all-to-all | bytes 589824 | tf_op jit(solution)/shard_map/all_to_all | solution.py:232
  68.4 1.2 %place.1 = f32[1,16,2,24,192]{4,3,2,1,0:T(8,128)} custom-call(bf16[384,384]{1,0:T(8,128)(2,1)S(1)} %bitcast.6), custom_call_target="tpu_custom_call" | custom-call | tf_op jit(solution)/shard_map/place/pallas_call | solution.py:233
  (1 shorter events, 0.0 us)
Async XLA Ops:
  2.7 3.3 %collective-permute-start = (bf16[192,384]{1,0:T(8,128)(2,1)S(1)}, bf16[192,384]{1,0:T(8,128)(2,1)S(1)}, u32[]{:S(2)}, u32[]{:S(2)}) collective-permute-start(bf16[192,384]{1,0:T(8,128)(2,1)S(1)} %get-tuple-element.12), channel_id=1, source_target_pairs={{0,1},{1,0},{2,3},{3,2},{4,5},{5,4},{6,7},{7,6},{8,9},{9,8},{10,11... | collective-permute-start | bytes 442376 | tf_op jit(solution)/shard_map/ppermute | solution.py:212

commit v4 on v3

--- a/solution.py
+++ b/solution.py
@@ -33,7 +33,7 @@
 
 def triple_kernel(
     retarded_ref, self_energy_ref, energy_ref, table_ref, own_ref, away_ref, energy_out_ref, table_out_ref,
-    green_ref, sigma_ref, left_ref, right_ref, sems, *, sizes
+    green_ref, sigma_ref, sems, *, sizes
 ):
     tile_count, hop_count = sizes
     energies, _, order, _ = green_ref.shape
@@ -56,51 +56,37 @@
     )
     for copy in copies[energies]:
         copy.start()
-    target = lax.broadcasted_iota(jnp.int32, (order, order), 0)
-    source = lax.broadcasted_iota(jnp.int32, (order, order), 1)
-    away = jnp.where(target >= half, 1, 0)
-    device = target - away * half
-    to_core = core + away - 2 * core * away
-    row = (2 * (device & (hop_count - 1)) + to_core) * tile_count + (device >> (hop_count.bit_length() - 1))
-    pick = one_hot(source == row)
-    sums = []
+    conj = jnp.where(member == 0, 1.0, -1.0)
+    parts = []
     for e in range(energies):
         for copy in copies[e]:
             copy.wait()
-        green_re, green_im = green_ref[e, 0], green_ref[e, 1]
-        sigma_re, sigma_im = sigma_ref[e, 0], sigma_ref[e, 1]
-        cross_re = (dot(green_re, sigma_re) - dot(green_im, sigma_im)).astype(jnp.bfloat16)
-        cross_im = (dot(green_re, sigma_im) + dot(green_im, sigma_re)).astype(jnp.bfloat16)
-
-        def set_sides(left_re, left_im, right_re, right_im, conj):
-            left_ref[0], left_ref[1] = left_re, left_im
-            for side in range(2):
-                re, im = right_re[side * half : (side + 1) * half], right_im[side * half : (side + 1) * half]
-                right_ref[side, 0, :half], right_ref[side, 0, half:] = re, -im if conj else im
-                right_ref[side, 1, :half], right_ref[side, 1, half:] = im, re if conj else -re
-
-        @pl.when(member == 0)
-        def _():
-            set_sides(cross_re, cross_im, green_re, green_im, True)
-
-        @pl.when(member == 1)
-        def _():
-            set_sides(green_re, green_im, cross_re, cross_im, False)
-
-        left = [dot(pick, left_ref[part]).astype(jnp.bfloat16) for part in range(2)]
-        sums.append(
-            [dot_rows(left[0], right_ref[side, 0]) + dot_rows(left[1], right_ref[side, 1]) for side in range(2)]
+        green = green_ref[e].reshape(2 * order, order)
+        by_re, by_im = dot(green, sigma_ref[e, 0]), dot(green, sigma_ref[e, 1])
+        cross = jnp.concatenate([by_re[:order] - by_im[order:], by_im[:order] + by_re[order:]], axis=0)
+        cross = cross.astype(jnp.bfloat16)
+        left, right = lax.select(member == 0, cross, green), lax.select(member == 0, green, cross)
+        by_re, by_im = dot_rows(left, right[:order]), dot_rows(left, right[order:])
+        parts.append((by_re[:order] + by_im[order:], (by_re[order:] - by_im[:order]) * conj))
+
+    def rows_of(array, core):
+        runs = [array[(2 * hop + core) * tile_count : (2 * hop + core + 1) * tile_count] for hop in range(hop_count)]
+        return jnp.concatenate(runs, axis=0).astype(jnp.bfloat16)
+
+    by_core = [[[rows_of(part, c) for part in pair] for pair in parts] for c in range(2)]
+    for side in range(2):
+        first, second = (
+            jnp.concatenate([part[:, side * half : (side + 1) * half] for pair in rows for part in pair], axis=1)
+            for rows in by_core
         )
-    for start, out_ref in ((0, own_ref), (half, away_ref)):
-        for side in range(2):
-            out_ref[side * half : (side + 1) * half] = jnp.concatenate(
-                [sums[e][side][start : start + half] for e in range(energies)], axis=1
-            ).astype(jnp.bfloat16)
+        own_ref[side * half : (side + 1) * half] = lax.select(core == 0, first, second)
+        away_ref[side * half : (side + 1) * half] = lax.select(core == 0, second, first)
     for copy in copies[energies]:
         copy.wait()
 
 
-def pick_kernel(energy_ref, out_ref):
+def pick_kernel(energy_ref, out_ref, *, sizes):
+    tile_count, hop_count = sizes
     energies, count, devices = out_ref.shape
     core = lax.axis_index("core")
     slots = jnp.concatenate([energy_ref[r : r + 1] for r in range(energy_ref.shape[0])], axis=1)
@@ -109,7 +95,10 @@
     slot = lax.broadcasted_iota(jnp.int32, (count, devices), 0)
     device = lax.broadcasted_iota(jnp.int32, (count, devices), 1)
     side = device & 1
-    first = ((device >> 1) * 2 + side + core - 2 * side * core) * energies
+    place = device >> 1
+    hop = sum(jnp.where(place >= n * tile_count, 1, 0) for n in range(1, hop_count)) if hop_count > 1 else 0
+    place = (place - hop * tile_count) * hop_count + hop
+    first = (place * 2 + side + core - 2 * side * core) * energies
     for e in range(energies):
         taken = dot(digits, one_hot(slot == first + e))
         out_ref[e] = one_hot(slot == (2.0 * taken[:1] + taken[1:2]).astype(jnp.int32))
@@ -121,20 +110,18 @@
     return left_re * right_re - left_im * right_im, left_re * right_im + left_im * right_re
 
 
-def correlate_kernel(signal_ref, pick_ref, table_ref, out_ref, *, scale):
+def correlate_kernel(signal_ref, pick_ref, table_ref, out_ref, ordered_ref, *, scale):
     energies, count, devices = pick_ref.shape
     half = signal_ref.shape[1] // (2 * energies)
-    gap = jnp.zeros((devices, LANES - half), jnp.bfloat16)
+    ordered_ref[...] = jnp.zeros(ordered_ref.shape, ordered_ref.dtype)
     sums = []
     for component in range(2):
         signal = signal_ref[component * devices : (component + 1) * devices]
-        ordered = None
-        for e in range(energies):
-            re, im = (signal[:, (2 * e + part) * half : (2 * e + part + 1) * half] for part in range(2))
-            term = dot(pick_ref[e], jnp.concatenate([re, gap, im, gap], axis=1))
-            ordered = term if ordered is None else ordered + term
-        ordered = ordered.astype(jnp.bfloat16)
-        sums.append([dot(table_ref[r * count : (r + 1) * count], ordered) for r in range(2)])
+        for part in range(2):
+            starts = [(2 * e + part) * half for e in range(energies)]
+            total = sum(dot(pick_ref[e], signal[:, start : start + half]) for e, start in enumerate(starts))
+            ordered_ref[component, :, part * LANES : part * LANES + half] = total.astype(jnp.bfloat16)
+        sums.append([dot(table_ref[r * count : (r + 1) * count], ordered_ref[component]) for r in range(2)])
     (one_cos, one_sin), (two_cos, two_sin) = sums
     even_parts = [a + b for a, b in zip(times(one_cos, two_cos), times(one_sin, two_sin))]
     odd_parts = [a - b for a, b in zip(times(one_sin, two_cos), times(one_cos, two_sin))]
@@ -202,8 +189,6 @@
         scratch_shapes=[
             pltpu.VMEM((energies, 2, order, order), jnp.bfloat16),
             pltpu.VMEM((energies, 2, order, order), jnp.bfloat16),
-            pltpu.VMEM((2, order, order), jnp.bfloat16),
-            pltpu.VMEM((2, 2, order, order), jnp.bfloat16),
             pltpu.SemaphoreType.DMA((energies + 1, 2)),
         ],
         interpret=INTERPRET,
@@ -211,7 +196,7 @@
     )(retarded, self_energy, slot_energy, table)
     sibling = lax.ppermute(away, "core", [(0, 1), (1, 0)])
     picks = pl.pallas_call(
-        pick_kernel,
+        functools.partial(pick_kernel, sizes=sizes),
         out_shape=on_chip_out((energies, slot_count, slot_count // energies), jnp.bfloat16),
         in_specs=[in_vmem],
         out_specs=in_vmem,
@@ -219,12 +204,13 @@
         name="picks",
     )(on_chip(slot_energy))
     blocks, picks = lax.optimization_barrier((jnp.stack([own, sibling], axis=1), picks))
-    gathered = lax.all_to_all(blocks, ("mem", "tile", "zh"), split_axis=0, concat_axis=0, tiled=True)
+    gathered = lax.all_to_all(blocks, ("mem", "zh", "tile"), split_axis=0, concat_axis=0, tiled=True)
     polar = pl.pallas_call(
         functools.partial(correlate_kernel, scale=2.0 / (2 * slot_count * math.sqrt(slot_count))),
         out_shape=on_chip_out((2, slot_count // 2, 4 * half), jnp.bfloat16),
         in_specs=[in_vmem] * 3,
         out_specs=in_vmem,
+        scratch_shapes=[pltpu.VMEM((2, slot_count, 2 * LANES), jnp.bfloat16)],
         interpret=INTERPRET,
         name="correlate",
     )(on_chip(gathered.reshape(2 * order, 2 * energies * half)), on_chip(picks), on_chip(table))

time: 69.8 us -> 69.1 us (0.990)
  the two profiles are of different devices: /device:TPU:4 before, /device:TPU:8 now
where the time goes in v4:
time: 69.1 us; the launch traced here: 68.8 us
  blocking collectives  59.6 us (86%)
  Pallas kernels  5.81 us (8%)
  starting transfers between devices  1.92 us (3%)
  waiting for transfers between devices  1 us (1%)
    all_to_all x1, blocking collectives, body(): lax.all_to_all(blocks, ('mem', 'zh', 'tile'), split_axis=0, concat_axis=0...  43.5 us
    all_to_all x1, blocking collectives, body(): lax.all_to_all(packed, ('mem', 'tile'), split_axis=0, concat_axis=0, tile...  16.1 us
    pallas_call x1, Pallas kernels, body(): pl.pallas_call(functools.partial(triple_kernel, sizes=sizes), out_shape=(...  2.49 us
    ppermute x1, starting transfers between devices, body(): sibling = lax.ppermute(away, 'core', [(0, 1), (1, 0)])  1.92 us
    pallas_call x1, Pallas kernels, body(): pl.pallas_call(functools.partial(correlate_kernel, scale=2.0 / (2 * slot_...  1.79 us
  transfers between devices with their start and end apart: 1, of which 1 were waited for; matrix products, arithmetic and copies ran while one was open for 0% of the time, Pallas kernels for 0%

profile of v4, /device:TPU:8, one launch (start us, length us, event | category | flops | bytes accessed | tf_op | source)
XLA Modules:
  0.0 68.8 jit_solution(906671846574660740)
XLA Ops:
  0.0 2.5 %triple.1 = (bf16[192,384]{1,0:T(8,128)(2,1)S(1)}, bf16[192,384]{1,0:T(8,128)(2,1)S(1)}, s32[3,128]{1,0:T(4,128)S(1)}, bf16[1536,384]{1,0:T(8,128)(2,1)S(1)}) custom-call(bf16[2,2,2,192,192]{4,3,2,1,0:T(8,128)(2,1)} %retarded_ref.1, bf16[1,2,2,192,192]{4,3,2,1,0:T(8,128)(2,1)} %self_energy_ref.1, s32[3,128]{1,0:T(4,128)} %bitcast.9, ...), custom_call_target="tpu_custom_call" | custom-call | tf_op jit(solution)/shard_map/triple/pallas_call | solution.py:184
  2.5 1.9 %collective-permute-start = (bf16[192,384]{1,0:T(8,128)(2,1)S(1)}, bf16[192,384]{1,0:T(8,128)(2,1)S(1)}, u32[]{:S(2)}, u32[]{:S(2)}) collective-permute-start(bf16[192,384]{1,0:T(8,128)(2,1)S(1)} %get-tuple-element.12), channel_id=1, source_target_pairs={{0,1},{1,0},{2,3},{3,2},{4,5},{5,4},{6,7},{7,6},{8,9},{9,8},{10,11... | collective-permute-start | bytes 442376 | tf_op jit(solution)/shard_map/ppermute | solution.py:197
  4.4 0.3 picks.1.pick_ref
  4.8 1.0 %collective-permute-done = bf16[192,384]{1,0:T(8,128)(2,1)S(1)} collective-permute-done((bf16[192,384]{1,0:T(8,128)(2,1)S(1)}, bf16[192,384]{1,0:T(8,128)(2,1)S(1)}, u32[]{:S(2)}, u32[]{:S(2)}) %collective-permute-start) | collective-permute-done | bytes 147488 | tf_op jit(solution)/shard_map/ppermute | solution.py:197
  5.8 0.3 copy.6
  6.1 43.5 %all_to_all.10 = bf16[192,2,384]{2,1,0:T(2,128)(2,1)S(1)} all-to-all(bf16[192,2,384]{2,1,0:T(2,128)(2,1)S(1)} %copy.6), channel_id=1, replica_groups=mesh['pair'=2,'mem'=2,'tile'=24,'zh'=4,'core'=2] {'mem','zh','tile'}, dimensions={0} | all-to-all | bytes 589824 | tf_op jit(solution)/shard_map/all_to_all | solution.py:207
  49.6 0.1 reshape.13.signal_ref
  49.7 1.8 %correlate.1 = bf16[2,192,384]{2,1,0:T(8,128)(2,1)S(1)} custom-call(bf16[384,384]{1,0:T(8,128)(2,1)S(1)} %reshape.13.signal_ref, bf16[2,384,192]{2,1,0:T(8,128)(2,1)S(1)} %picks.1.pick_ref, bf16[1536,384]{1,0:T(8,128)(2,1)S(1)} %get-tuple-element.16.table_ref), custom_call_target="tpu_custom_call" | custom-call | tf_op jit(solution)/shard_map/correlate/pallas_call | solution.py:208
  51.5 16.1 %all_to_all.11 = bf16[48,8,384]{2,1,0:T(8,128)(2,1)S(1)} all-to-all(bf16[48,8,384]{2,1,0:T(8,128)(2,1)S(1)} %bitcast.5), channel_id=1, replica_groups=mesh['pair'=2,'mem'=2,'tile'=24,'zh'=4,'core'=2] {'mem','tile'}, dimensions={0} | all-to-all | bytes 589824 | tf_op jit(solution)/shard_map/all_to_all | solution.py:218
  67.6 1.2 %place.1 = f32[1,16,2,24,192]{4,3,2,1,0:T(8,128)} custom-call(bf16[384,384]{1,0:T(8,128)(2,1)S(1)} %bitcast.6), custom_call_target="tpu_custom_call" | custom-call | tf_op jit(solution)/shard_map/place/pallas_call | solution.py:219
  (1 shorter events, 0.0 us)
Async XLA Ops:
  2.5 3.3 %collective-permute-start = (bf16[192,384]{1,0:T(8,128)(2,1)S(1)}, bf16[192,384]{1,0:T(8,128)(2,1)S(1)}, u32[]{:S(2)}, u32[]{:S(2)}) collective-permute-start(bf16[192,384]{1,0:T(8,128)(2,1)S(1)} %get-tuple-element.12), channel_id=1, source_target_pairs={{0,1},{1,0},{2,3},{3,2},{4,5},{5,4},{6,7},{7,6},{8,9},{9,8},{10,11... | collective-permute-start | bytes 442376 | tf_op jit(solution)/shard_map/ppermute | solution.py:197

commit v5 on v4

--- a/solution.py
+++ b/solution.py
@@ -57,14 +57,17 @@
     for copy in copies[energies]:
         copy.start()
     conj = jnp.where(member == 0, 1.0, -1.0)
-    parts = []
     for e in range(energies):
         for copy in copies[e]:
             copy.wait()
-        green = green_ref[e].reshape(2 * order, order)
-        by_re, by_im = dot(green, sigma_ref[e, 0]), dot(green, sigma_ref[e, 1])
-        cross = jnp.concatenate([by_re[:order] - by_im[order:], by_im[:order] + by_re[order:]], axis=0)
-        cross = cross.astype(jnp.bfloat16)
+    greens = [green_ref[e].reshape(2 * order, order) for e in range(energies)]
+    first = [[dot(greens[e], sigma_ref[e, part]) for part in range(2)] for e in range(energies)]
+    crosses = [
+        jnp.concatenate([by_re[:order] - by_im[order:], by_im[:order] + by_re[order:]], axis=0).astype(jnp.bfloat16)
+        for by_re, by_im in first
+    ]
+    parts = []
+    for green, cross in zip(greens, crosses):
         left, right = lax.select(member == 0, cross, green), lax.select(member == 0, green, cross)
         by_re, by_im = dot_rows(left, right[:order]), dot_rows(left, right[order:])
         parts.append((by_re[:order] + by_im[order:], (by_re[order:] - by_im[:order]) * conj))
@@ -85,56 +88,66 @@
         copy.wait()
 
 
-def pick_kernel(energy_ref, out_ref, *, sizes):
+def arrange_kernel(energy_ref, table_ref, out_ref, pick_ref, *, sizes):
     tile_count, hop_count = sizes
-    energies, count, devices = out_ref.shape
+    count = pick_ref.shape[0]
+    energies = count // (2 * tile_count * hop_count)
+    devices = count // energies
     core = lax.axis_index("core")
     slots = jnp.concatenate([energy_ref[r : r + 1] for r in range(energy_ref.shape[0])], axis=1)
     digit = lax.broadcasted_iota(jnp.int32, (16, count), 0)
     digits = jnp.where(digit == 0, slots >> 1, slots & 1).astype(jnp.float32).astype(jnp.bfloat16)
-    slot = lax.broadcasted_iota(jnp.int32, (count, devices), 0)
-    device = lax.broadcasted_iota(jnp.int32, (count, devices), 1)
-    side = device & 1
-    place = device >> 1
-    hop = sum(jnp.where(place >= n * tile_count, 1, 0) for n in range(1, hop_count)) if hop_count > 1 else 0
+    column = lax.broadcasted_iota(jnp.int32, (1, count), 1)
+    energy = sum((jnp.where(column >= n * devices, 1, 0) for n in range(1, energies)), jnp.zeros_like(column))
+    device = column - energy * devices
+    side, place = device & 1, device >> 1
+    hop = sum((jnp.where(place >= n * tile_count, 1, 0) for n in range(1, hop_count)), jnp.zeros_like(column))
     place = (place - hop * tile_count) * hop_count + hop
-    first = (place * 2 + side + core - 2 * side * core) * energies
-    for e in range(energies):
-        taken = dot(digits, one_hot(slot == first + e))
-        out_ref[e] = one_hot(slot == (2.0 * taken[:1] + taken[1:2]).astype(jnp.int32))
+    wanted = (place * 2 + side + core - 2 * side * core) * energies + energy
+    row = lax.broadcasted_iota(jnp.int32, (count, count), 0)
+    taken = dot(digits, one_hot(row == wanted))
+    pick_ref[...] = one_hot(row == (2.0 * taken[:1] + taken[1:2]).astype(jnp.int32))
+    out_ref[...] = dot(table_ref[: 2 * count], pick_ref[...]).astype(jnp.bfloat16)
 
 
 def times(left, right):
-    left_re, left_im = left[:, :LANES], left[:, LANES:]
-    right_re, right_im = right[:, :LANES], right[:, LANES:]
-    return left_re * right_re - left_im * right_im, left_re * right_im + left_im * right_re
-
-
-def correlate_kernel(signal_ref, pick_ref, table_ref, out_ref, ordered_ref, *, scale):
-    energies, count, devices = pick_ref.shape
+    return left[0] * right[0] - left[1] * right[1], left[0] * right[1] + left[1] * right[0]
+
+
+def correlate_kernel(signal_ref, forward_ref, table_ref, out_ref, staged_ref):
+    _, count, _ = staged_ref.shape
+    devices = signal_ref.shape[0] // 2
+    energies = count // devices
     half = signal_ref.shape[1] // (2 * energies)
-    ordered_ref[...] = jnp.zeros(ordered_ref.shape, ordered_ref.dtype)
-    sums = []
+    staged_ref[...] = jnp.zeros(staged_ref.shape, staged_ref.dtype)
     for component in range(2):
         signal = signal_ref[component * devices : (component + 1) * devices]
-        for part in range(2):
-            starts = [(2 * e + part) * half for e in range(energies)]
-            total = sum(dot(pick_ref[e], signal[:, start : start + half]) for e, start in enumerate(starts))
-            ordered_ref[component, :, part * LANES : part * LANES + half] = total.astype(jnp.bfloat16)
-        sums.append([dot(table_ref[r * count : (r + 1) * count], ordered_ref[component]) for r in range(2)])
-    (one_cos, one_sin), (two_cos, two_sin) = sums
-    even_parts = [a + b for a, b in zip(times(one_cos, two_cos), times(one_sin, two_sin))]
-    odd_parts = [a - b for a, b in zip(times(one_sin, two_cos), times(one_cos, two_sin))]
+        for e in range(energies):
+            for part in range(2):
+                start = (2 * e + part) * half
+                staged_ref[component, e * devices : (e + 1) * devices, part * LANES : part * LANES + half] = signal[
+                    :, start : start + half
+                ]
+    spectra = []
+    for component in range(2):
+        cos_sum, sin_sum = (dot(forward_ref[r * count : (r + 1) * count], staged_ref[component]) for r in range(2))
+        turned = (sin_sum[:, LANES:], -sin_sum[:, :LANES])
+        plain = (cos_sum[:, :LANES], cos_sum[:, LANES:])
+        spectra.append([[p + t for p, t in zip(plain, turned)], [p - t for p, t in zip(plain, turned)]])
+    one, two = spectra
+    ahead, behind = times(one[0], two[1]), times(one[1], two[0])
+    even_parts = [ahead[0] + behind[0], ahead[1] + behind[1]]
+    odd_parts = [behind[1] - ahead[1], ahead[0] - behind[0]]
     even = dot(table_ref[2 * count : 3 * count], jnp.concatenate(even_parts, axis=1).astype(jnp.bfloat16))
     odd = dot(table_ref[3 * count :], jnp.concatenate(odd_parts, axis=1).astype(jnp.bfloat16))
     rows = count // 2
     for component, total in enumerate((even + odd, even - odd)):
-        re = total[:, LANES : LANES + half] * scale
-        im = total[:, :half] * -scale
-        out_ref[component] = jnp.concatenate([re[:rows], im[:rows], re[rows:], im[rows:]], axis=1).astype(out_ref.dtype)
-
-
-def place_kernel(gathered_ref, out_ref, placed_ref, sems):
+        total = total.astype(out_ref.dtype)
+        im, re = total[:, LANES : LANES + half], total[:, :half]
+        out_ref[component] = jnp.concatenate([im[:rows], re[:rows], im[rows:], re[rows:]], axis=1)
+
+
+def place_kernel(gathered_ref, out_ref, placed_ref, sems, *, scale):
     _, lags, _, tiles, order = out_ref.shape
     half, low = order // 2, lags // 2
     rows = low * tiles
@@ -146,7 +159,7 @@
         for part in range(2):
             lane = (2 * high + part) * half
             both = [gathered_ref[side * rows : (side + 1) * rows, lane : lane + half] for side in range(2)]
-            moved = dot(pick, jnp.concatenate(both, axis=1))
+            moved = dot(pick, jnp.concatenate(both, axis=1)) * (-scale if part else scale)
             for lag in range(low):
                 placed_ref[high, part, lag] = moved[lag * tiles : (lag + 1) * tiles]
             copies.append(
@@ -195,29 +208,30 @@
         name="triple",
     )(retarded, self_energy, slot_energy, table)
     sibling = lax.ppermute(away, "core", [(0, 1), (1, 0)])
-    picks = pl.pallas_call(
-        functools.partial(pick_kernel, sizes=sizes),
-        out_shape=on_chip_out((energies, slot_count, slot_count // energies), jnp.bfloat16),
-        in_specs=[in_vmem],
+    forward = pl.pallas_call(
+        functools.partial(arrange_kernel, sizes=sizes),
+        out_shape=on_chip_out((2 * slot_count, slot_count), jnp.bfloat16),
+        in_specs=[in_vmem] * 2,
         out_specs=in_vmem,
+        scratch_shapes=[pltpu.VMEM((slot_count, slot_count), jnp.bfloat16)],
         interpret=INTERPRET,
         name="picks",
-    )(on_chip(slot_energy))
-    blocks, picks = lax.optimization_barrier((jnp.stack([own, sibling], axis=1), picks))
+    )(on_chip(slot_energy), on_chip(table))
+    blocks, forward = lax.optimization_barrier((jnp.stack([own, sibling], axis=1), forward))
     gathered = lax.all_to_all(blocks, ("mem", "zh", "tile"), split_axis=0, concat_axis=0, tiled=True)
     polar = pl.pallas_call(
-        functools.partial(correlate_kernel, scale=2.0 / (2 * slot_count * math.sqrt(slot_count))),
+        correlate_kernel,
         out_shape=on_chip_out((2, slot_count // 2, 4 * half), jnp.bfloat16),
         in_specs=[in_vmem] * 3,
         out_specs=in_vmem,
         scratch_shapes=[pltpu.VMEM((2, slot_count, 2 * LANES), jnp.bfloat16)],
         interpret=INTERPRET,
         name="correlate",
-    )(on_chip(gathered.reshape(2 * order, 2 * energies * half)), on_chip(picks), on_chip(table))
+    )(on_chip(gathered.reshape(2 * order, 2 * energies * half)), on_chip(forward), on_chip(table))
     packed = polar.reshape(2 * tile_count, lag_count // 2, 4 * half)
     regrouped = lax.all_to_all(packed, ("mem", "tile"), split_axis=0, concat_axis=0, tiled=True)
     return pl.pallas_call(
-        place_kernel,
+        functools.partial(place_kernel, scale=1.0 / (2 * slot_count * math.sqrt(slot_count))),
         out_shape=jax.ShapeDtypeStruct((1, lag_count, 2, tile_count, order), jnp.float32),
         in_specs=[in_vmem],
         out_specs=in_place,

time: 69.1 us -> 68 us (0.984)
  transfers between devices with their start and end apart: 1 -> 1, of which waited for: 1 -> 1; matrix products, arithmetic and copies ran while one was open for 0% -> 0% of each run, Pallas kernels for 0% -> 1%
where the time goes in v5:
time: 68 us; the launch traced here: 67.8 us
  blocking collectives  59.6 us (88%)
  Pallas kernels  5.12 us (8%)
  starting transfers between devices  1.92 us (3%)
    all_to_all x1, blocking collectives, body(): lax.all_to_all(blocks, ('mem', 'zh', 'tile'), split_axis=0, concat_axis=0...  43.5 us
    all_to_all x1, blocking collectives, body(): lax.all_to_all(packed, ('mem', 'tile'), split_axis=0, concat_axis=0, tile...  16.1 us
    pallas_call x1, Pallas kernels, body(): pl.pallas_call(functools.partial(triple_kernel, sizes=sizes), out_shape=(...  2.08 us
    ppermute x1, starting transfers between devices, body(): sibling = lax.ppermute(away, 'core', [(0, 1), (1, 0)])  1.92 us
  transfers between devices with their start and end apart: 1, of which 1 were waited for; matrix products, arithmetic and copies ran while one was open for 0% of the time, Pallas kernels for 1%

profile of v5, /device:TPU:8, one launch (start us, length us, event | category | flops | bytes accessed | tf_op | source)
XLA Modules:
  0.0 67.8 jit_solution(7390137112336989201)
XLA Ops:
  0.0 2.1 %triple.1 = (bf16[192,384]{1,0:T(8,128)(2,1)S(1)}, bf16[192,384]{1,0:T(8,128)(2,1)S(1)}, s32[3,128]{1,0:T(4,128)S(1)}, bf16[1536,384]{1,0:T(8,128)(2,1)S(1)}) custom-call(bf16[2,2,2,192,192]{4,3,2,1,0:T(8,128)(2,1)} %retarded_ref.1, bf16[1,2,2,192,192]{4,3,2,1,0:T(8,128)(2,1)} %self_energy_ref.1, s32[3,128]{1,0:T(4,128)} %bitcast.9, ...), custom_call_target="tpu_custom_call" | custom-call | tf_op jit(solution)/shard_map/triple/pallas_call | solution.py:197
  2.1 1.9 %collective-permute-start = (bf16[192,384]{1,0:T(8,128)(2,1)S(1)}, bf16[192,384]{1,0:T(8,128)(2,1)S(1)}, u32[]{:S(2)}, u32[]{:S(2)}) collective-permute-start(bf16[192,384]{1,0:T(8,128)(2,1)S(1)} %get-tuple-element.12), channel_id=1, source_target_pairs={{0,1},{1,0},{2,3},{3,2},{4,5},{5,4},{6,7},{7,6},{8,9},{9,8},{10,11... | collective-permute-start | bytes 442376 | tf_op jit(solution)/shard_map/ppermute | solution.py:210
  4.0 0.7 %picks.1.forward_ref = bf16[768,384]{1,0:T(8,128)(2,1)S(1)} custom-call(s32[3,128]{1,0:T(4,128)S(1)} %get-tuple-element.13.energy_ref, bf16[1536,384]{1,0:T(8,128)(2,1)S(1)} %get-tuple-element.14.table_ref), custom_call_target="tpu_custom_call" | custom-call | tf_op jit(solution)/shard_map/picks/pallas_call | solution.py:211
  4.7 0.6 collective-permute-done
  5.4 0.3 copy.6
  5.7 43.5 %all_to_all.10 = bf16[192,2,384]{2,1,0:T(2,128)(2,1)S(1)} all-to-all(bf16[192,2,384]{2,1,0:T(2,128)(2,1)S(1)} %copy.6), channel_id=1, replica_groups=mesh['pair'=2,'mem'=2,'tile'=24,'zh'=4,'core'=2] {'mem','zh','tile'}, dimensions={0} | all-to-all | bytes 589824 | tf_op jit(solution)/shard_map/all_to_all | solution.py:221
  49.2 0.1 reshape.13.signal_ref
  49.3 1.1 %correlate.1 = bf16[2,192,384]{2,1,0:T(8,128)(2,1)S(1)} custom-call(bf16[384,384]{1,0:T(8,128)(2,1)S(1)} %reshape.13.signal_ref, bf16[768,384]{1,0:T(8,128)(2,1)S(1)} %picks.1.forward_ref, bf16[1536,384]{1,0:T(8,128)(2,1)S(1)} %get-tuple-element.14.table_ref), custom_call_target="tpu_custom_call" | custom-call | tf_op jit(solution)/shard_map/correlate/pallas_call | solution.py:222
  50.4 16.1 %all_to_all.11 = bf16[48,8,384]{2,1,0:T(8,128)(2,1)S(1)} all-to-all(bf16[48,8,384]{2,1,0:T(8,128)(2,1)S(1)} %bitcast.5), channel_id=1, replica_groups=mesh['pair'=2,'mem'=2,'tile'=24,'zh'=4,'core'=2] {'mem','tile'}, dimensions={0} | all-to-all | bytes 589824 | tf_op jit(solution)/shard_map/all_to_all | solution.py:232
  66.5 1.2 %place.1 = f32[1,16,2,24,192]{4,3,2,1,0:T(8,128)} custom-call(bf16[384,384]{1,0:T(8,128)(2,1)S(1)} %bitcast.6), custom_call_target="tpu_custom_call" | custom-call | tf_op jit(solution)/shard_map/place/pallas_call | solution.py:233
  (1 shorter events, 0.0 us)
Async XLA Ops:
  2.1 3.3 %collective-permute-start = (bf16[192,384]{1,0:T(8,128)(2,1)S(1)}, bf16[192,384]{1,0:T(8,128)(2,1)S(1)}, u32[]{:S(2)}, u32[]{:S(2)}) collective-permute-start(bf16[192,384]{1,0:T(8,128)(2,1)S(1)} %get-tuple-element.12), channel_id=1, source_target_pairs={{0,1},{1,0},{2,3},{3,2},{4,5},{5,4},{6,7},{7,6},{8,9},{9,8},{10,11... | collective-permute-start | bytes 442376 | tf_op jit(solution)/shard_map/ppermute | solution.py:210
